TPU v7x, 768 devices: a whole 4x8x12 slice. The times are simulated.
768 devices in a mesh: section: 24 (over z_lo, x, core), tp: 32 (over y, z_hi).
Axes of the slice: x: 4, y: 8, z: 12 (z_hi: 4, z_lo: 3; z = z_hi * 3 + z_lo), core: 2. Of those that a mesh axis runs over, the one named last changes fastest.
Arguments:
- inputs: bfloat16 [24, 128, 2560], P('section', 'tp'), may hold values from -6 to 6
- out_grad: bfloat16 [24, 128, 2560], P('section', 'tp'), may hold values from -6 to 6
- w_gate: bfloat16 [2560, 13824], P(None, 'tp'), may hold values from -0.125 to 0.125
- w_up: bfloat16 [2560, 13824], P(None, 'tp'), may hold values from -0.125 to 0.125
- w_down: bfloat16 [13824, 2560], P('tp'), may hold values from -0.125 to 0.125
Outputs:
- received: bfloat16 [24, 128, 2560], P('section', 'tp')
All inputs are finite; a program needn't handle non-finite values.
Results may differ from a plain program's by a relative error of at most 0.0049.
Values may be sent and summed in bfloat16 or wider, within the bound.
No kernel may reach another device: no remote copies, remote signals or barrier semaphores. Data moves between devices by JAX's collectives and lax.ppermute only.
A program may use at most 32 MiB of HBM per device.

v0:
```python
import jax
import jax.numpy as jnp
from jax import lax
from jax.sharding import PartitionSpec as P


def passed_along(block, axis, distance):
    devices = range(lax.axis_size(axis))
    route = [(i - distance, i) for i in devices if i - distance in devices]
    return lax.ppermute(block, axis, route)


def hidden_grads(piece, w_gate, w_up, w_down):
    gate = jnp.dot(piece[0], w_gate, preferred_element_type=jnp.float32)
    up = jnp.dot(piece[0], w_up, preferred_element_type=jnp.float32)
    hid_grad = lax.dot_general(
        piece[1], w_down, (((1,), (1,)), ((), ())), preferred_element_type=jnp.float32
    )
    sig = jax.nn.sigmoid(gate)
    up_grad = (hid_grad * gate * sig).astype(jnp.bfloat16)
    gate_grad = (hid_grad * up * sig * (1.0 + gate * (1.0 - sig))).astype(jnp.bfloat16)
    return jnp.stack([gate_grad, up_grad], axis=0)


def on_device(inputs, out_grad, w_gate, w_up, w_down):
    stacked = jnp.stack([inputs[0], out_grad[0]], axis=0)
    gathered = lax.all_gather(stacked, "tp", axis=1, tiled=True)
    grads = hidden_grads(gathered, w_gate, w_up, w_down)
    gate_rows = grads[0]
    up_rows = grads[1]
    total = lax.dot_general(
        gate_rows, w_gate, (((1,), (1,)), ((), ())), preferred_element_type=jnp.float32
    )
    in_grad = lax.psum_scatter(
        total
        + lax.dot_general(
            up_rows, w_up, (((1,), (1,)), ((), ())), preferred_element_type=jnp.float32
        ),
        "tp",
        scatter_dimension=0,
        tiled=True,
    ).astype(jnp.bfloat16)
    received = passed_along(in_grad, "section", -1)
    return received[None]


def solution(mesh):
    placed = (
        P("section", "tp", None),
        P("section", "tp", None),
        P(None, "tp"),
        P(None, "tp"),
        P("tp", None),
    )
    return jax.shard_map(
        on_device, mesh=mesh, in_specs=placed, out_specs=P("section", "tp", None), check_vma=False
    )
```

profile of v0, /device:TPU:1, one launch (start us, length us, event | category | flops | bytes accessed | tf_op | source)
XLA Modules:
  0.0 334.4 jit_solution(13551236404253448168)
XLA Ops:
  6.5 0.0 copy-start
  6.5 0.0 all-gather.2.cloned.1.call-start
  6.5 0.9 copy.8
  7.5 0.8 copy.9
  8.2 0.7 pad_maximum_fusion
  8.9 0.0 all-gather.2.cloned.1.call-update
  9.0 1.3 dynamic-slice
  10.9 99.2 %all-gather.2.cloned.1.call-done = bf16[2,128,2560]{2,0,1:T(2,128)(2,1)} async-done(((bf16[2,4,2560]{2,0,1:T(2,128)(2,1)}), bf16[2,128,2560]{2,0,1:T(2,128)(2,1)}) %all-gather.2.cloned.1.call-update) | async-done | bytes 1310736 | tf_op jit(solution)/shard_map/all_gather | solution.py:27
  110.0 0.0 copy-start.1
  110.0 4.2 %fusion.13 = (bf16[1,128,2560]{2,0,1:T(2,128)(2,1)S(1)}, bf16[1,128,2560]{2,0,1:T(2,128)(2,1)S(1)}) fusion(bf16[2,128,2560]{2,0,1:T(2,128)(2,1)} %all-gather.2.cloned.1.call-done), kind=kLoop, calls=%fused_computation.21 | loop fusion | bytes 2621440 | tf_op jit(solution)/shard_map/slice | solution.py:15
  114.2 0.0 copy-start.2
  114.2 0.0 copy-start.3
  114.2 0.0 copy-done.1
  114.2 1.4 fusion.5
  115.7 0.0 copy-done.2
  115.7 0.7 copy-done.3
  116.4 1.4 fusion.4
  117.8 0.0 copy-done
  117.8 4.1 %fusion.3 = f32[128,2560]{1,0:T(8,128)S(1)} fusion(bf16[2560,432]{0,1:T(8,128)(2,1)} %param.7, f32[128,432]{0,1:T(8,128)} %fusion.4, bf16[2560,432]{0,1:T(8,128)(2,1)S(1)} %copy-done, bf16[1,128,2560]{2,0,1:T(2,128)(2,1)} %copy-done.2, f32[128,432]{0,1:T(8,128)} %fusion.5), kind=kOutput, calls=%fused_computation.5 | convolution fusion | flops 566784000 | bytes 6832128 | tf_op jit(solution)/shard_map/dot_general | solution.py:31
  121.9 2.7 convolution_add_fusion
  124.6 165.2 %all-reduce.2 = bf16[128,2560]{1,0:T(8,128)(2,1)S(1)} all-reduce(f32[128,2560]{1,0:T(8,128)} %convolution_add_fusion), channel_id=2, replica_groups=mesh['section'=24,'tp'=32] {'tp'}, use_global_device_ids=true, to_apply=%region_0.0.clone | all-reduce | flops 327680 | bytes 1966080
  289.8 31.3 %collective-permute-start = (bf16[4,2560]{1,0:T(4,128)(2,1)S(1)}, bf16[4,2560]{1,0:T(4,128)(2,1)S(1)}, u32[]{:S(2)}, u32[]{:S(2)}) collective-permute-start(bf16[4,2560]{1,0:T(4,128)(2,1)S(1)} %dynamic-slice_convert_fusion), channel_id=1, source_target_pairs={{32,0},{64,32},{96,64},{128,96},{160,128},{192,160},{224,192},{256... | collective-permute-start | bytes 61448 | tf_op jit(solution)/shard_map/ppermute | solution.py:10
  321.1 5.8 %collective-permute-done = bf16[4,2560]{1,0:T(4,128)(2,1)S(1)} collective-permute-done((bf16[4,2560]{1,0:T(4,128)(2,1)S(1)}, bf16[4,2560]{1,0:T(4,128)(2,1)S(1)}, u32[]{:S(2)}, u32[]{:S(2)}) %collective-permute-start) | collective-permute-done | bytes 20512 | tf_op jit(solution)/shard_map/ppermute | solution.py:10
  327.0 0.6 copy.23
  (1 shorter events, 0.0 us)
Async XLA Ops:
  6.5 111.3 %copy-start = (bf16[2560,432]{0,1:T(8,128)(2,1)S(1)}, bf16[2560,432]{0,1:T(8,128)(2,1)}, u32[]{:S(2)}) copy-start(bf16[2560,432]{0,1:T(8,128)(2,1)} %param.8) | copy-start | bytes 6635524
  6.5 103.5 %all-gather.2.cloned.1.call-start = ((), (), s32[]{:S(2)}) async-start(), calls=%async_computation | async-start | bytes 1351680 | tf_op jit(solution)/shard_map/all_gather | solution.py:27
  110.0 4.2 %copy-start.1 = (bf16[2560,432]{0,1:T(8,128)(2,1)S(1)}, bf16[2560,432]{0,1:T(8,128)(2,1)}, u32[]{:S(2)}) copy-start(bf16[2560,432]{0,1:T(8,128)(2,1)} %param.7) | copy-start | bytes 6635524
  114.2 1.5 copy-start.2
  114.2 2.2 copy-start.3
  289.8 37.2 %collective-permute-start = (bf16[4,2560]{1,0:T(4,128)(2,1)S(1)}, bf16[4,2560]{1,0:T(4,128)(2,1)S(1)}, u32[]{:S(2)}, u32[]{:S(2)}) collective-permute-start(bf16[4,2560]{1,0:T(4,128)(2,1)S(1)} %dynamic-slice_convert_fusion), channel_id=1, source_target_pairs={{32,0},{64,32},{96,64},{128,96},{160,128},{192,160},{224,192},{256... | collective-permute-start | bytes 61448 | tf_op jit(solution)/shard_map/ppermute | solution.py:10
Sparse Core Ops, SparseCore 0:
  11.1 98.9 all-gather.1
where the time goes:
time: 335 us; the launch traced here: 334 us
  blocking collectives  165 us (49%)
  waiting for transfers between devices  105 us (31%)
  starting transfers between devices  31.3 us (9%)
  between operations  14.1 us (4%)
  matrix products  9.62 us (3%)
  local copies, waits for them, and re-layouts  8.49 us (3%)
    unnamed x1, blocking collectives  165 us
    all_gather x1, waiting for transfers between devices, on_device(): gathered = lax.all_gather(stacked, 'tp', axis=1, tiled=True)  99.2 us
    ppermute x1, starting transfers between devices, passed_along(): return lax.ppermute(block, axis, route)  31.3 us
  transfers between devices with their start and end apart: 2, of which 2 were waited for; matrix products, arithmetic and copies ran while one was open for 0% of the time, Pallas kernels for 0%

commit v1 on v0

v1 whole, which is shorter than its diff:
```python
import jax
import jax.numpy as jnp
from jax import lax
from jax.sharding import Mesh, PartitionSpec as P

TP = ("y", "zh")


def passed_along(block, axis, distance):
    devices = range(lax.axis_size(axis))
    route = [(i - distance, i) for i in devices if i - distance in devices]
    return lax.ppermute(block, axis, route)


def on_device(inputs, out_grad, w_gate, w_up, w_down):
    rows, width = inputs.shape[1:]
    ny, nz = lax.axis_size("y"), lax.axis_size("zh")
    both = jnp.concatenate([inputs[0], out_grad[0]], axis=0)
    near = lax.all_to_all(
        jnp.broadcast_to(both, (nz,) + both.shape), "zh", 0, 0, tiled=True
    )
    near = near.reshape(nz, 2, rows, width).transpose(1, 0, 2, 3)
    near = near.reshape(2 * nz * rows, width)
    far = lax.all_to_all(
        jnp.broadcast_to(near, (ny,) + near.shape), "y", 0, 0, tiled=True
    )
    x = far[:, : nz * rows].reshape(-1, width)
    g = far[:, nz * rows :].reshape(-1, width)
    gate = jnp.dot(x, w_gate, preferred_element_type=jnp.float32)
    up = jnp.dot(x, w_up, preferred_element_type=jnp.float32)
    hid_grad = lax.dot_general(
        g, w_down, (((1,), (1,)), ((), ())), preferred_element_type=jnp.float32
    )
    sig = jax.nn.sigmoid(gate)
    up_grad = (hid_grad * gate * sig).astype(jnp.bfloat16)
    gate_grad = (hid_grad * up * sig * (1.0 + gate * (1.0 - sig))).astype(jnp.bfloat16)
    total = lax.dot_general(
        gate_grad, w_gate, (((1,), (1,)), ((), ())), preferred_element_type=jnp.float32
    ) + lax.dot_general(
        up_grad, w_up, (((1,), (1,)), ((), ())), preferred_element_type=jnp.float32
    )
    parts = total.astype(jnp.bfloat16).reshape(ny * nz, rows, width)
    parts = lax.all_to_all(parts, TP, 0, 0, tiled=True)
    in_grad = jnp.sum(parts.astype(jnp.float32), axis=0).astype(jnp.bfloat16)
    return passed_along(in_grad, "section", -1)[None]


def solution(mesh):
    n_section, n_tp = mesh.devices.shape
    fine = Mesh(mesh.devices.reshape(n_section, 8, n_tp // 8), ("section",) + TP)
    placed = (
        P("section", TP, None),
        P("section", TP, None),
        P(None, TP),
        P(None, TP),
        P(TP, None),
    )
    return jax.shard_map(
        on_device, mesh=fine, in_specs=placed, out_specs=P("section", TP, None), check_vma=False
    )
```

time: 335 us -> 116 us (0.35)
  the two profiles are of different devices: /device:TPU:1 before, /device:TPU:79 now
where the time goes in v1:
time: 116 us
  blocking collectives  97.7 us (84%)
  matrix products  7.87 us (7%)
  waiting for transfers between devices  4.19 us (4%)
  starting transfers between devices  3.01 us (3%)
  local copies, waits for them, and re-layouts  1.95 us (2%)
  other arithmetic  1.2 us (1%)
    all_to_all x1, blocking collectives, on_device(): parts = lax.all_to_all(parts, TP, 0, 0, tiled=True)  40.1 us
    all_to_all x1, blocking collectives, on_device(): lax.all_to_all(jnp.broadcast_to(near, (ny,) + near.shape), 'y', 0, 0, til...  34.5 us
    all_to_all x1, blocking collectives, on_device(): lax.all_to_all(jnp.broadcast_to(both, (nz,) + both.shape), 'zh', 0, 0, ti...  23 us
    dot_general x1, matrix products, on_device(): lax.dot_general(gate_grad, w_gate, (((1,), (1,)), ((), ())), preferred_el...  4.54 us
    ppermute x1, waiting for transfers between devices, passed_along(): return lax.ppermute(block, axis, route)  4.19 us
    ppermute x1, starting transfers between devices, passed_along(): return lax.ppermute(block, axis, route)  3.01 us
  transfers between devices with their start and end apart: 1, of which 1 were waited for; matrix products, arithmetic and copies ran while one was open for 0% of the time, Pallas kernels for 0%

profile of v1, /device:TPU:79, one launch (start us, length us, event | category | flops | bytes accessed | tf_op | source)
XLA Modules:
  0.0 116.0 jit_solution(12550272420627464996)
XLA Ops:
  0.0 0.0 copy-start
  0.0 0.9 pad_maximum_fusion
  0.9 23.0 %all_to_all.15 = bf16[4,8,2560]{2,1,0:T(8,128)(2,1)S(1)} all-to-all(bf16[4,8,2560]{2,1,0:T(8,128)(2,1)S(1)} %broadcast_in_dim.9), channel_id=1, replica_groups=mesh['section'=24,'y'=8,'zh'=4] {'zh'}, dimensions={0} | all-to-all | bytes 327680 | tf_op jit(solution)/shard_map/all_to_all | solution.py:19
  24.0 0.1 copy.7
  24.1 0.1 copy.8
  24.2 0.1 broadcast_in_dim.10
  24.3 0.0 copy-start.2
  24.3 34.5 %all_to_all.16 = bf16[8,32,2560]{2,1,0:T(8,128)(2,1)S(1)} all-to-all(bf16[8,32,2560]{2,1,0:T(8,128)(2,1)S(1)} %broadcast_in_dim.10), channel_id=1, replica_groups=mesh['section'=24,'y'=8,'zh'=4] {'y'}, dimensions={0} | all-to-all | bytes 2621440 | tf_op jit(solution)/shard_map/all_to_all | solution.py:24
  58.8 0.0 copy-start.1
  58.8 0.1 fusion.12
  58.9 0.0 copy-done.2
  58.9 0.7 fusion.13
  59.7 0.8 copy-done.1
  60.5 0.7 fusion.14
  61.2 0.0 copy-done
  61.2 4.5 %fusion.4 = f32[128,2560]{1,0:T(8,128)} fusion(bf16[2560,432]{0,1:T(8,128)(2,1)} %param.7, f32[128,432]{0,1:T(8,128)S(1)} %fusion.13, bf16[128,2560]{1,0:T(8,128)(2,1)S(1)} %bitcast.17, bf16[2560,432]{0,1:T(8,128)(2,1)S(1)} %copy-done, f32[128,432]{0,1:T(8,128)S(1)} %fusion.14), kind=kOutput, calls=%fused_computation.6 | convolution fusion | flops 566784000 | bytes 6832128 | tf_op jit(solution)/shard_map/dot_general | solution.py:37
  65.7 1.9 %fusion = bf16[128,2560]{1,0:T(8,128)(2,1)S(1)} fusion(f32[128,2560]{1,0:T(8,128)} %fusion.4, bf16[2560,432]{0,1:T(8,128)(2,1)S(1)} %copy-done, f32[128,432]{0,1:T(8,128)S(1)} %fusion.13, f32[128,432]{0,1:T(8,128)S(1)} %fusion.14), kind=kOutput, calls=%fused_computation.1 | convolution fusion | flops 284102656 | bytes 4620288 | tf_op jit(solution)/shard_map/dot_general | solution.py:39
  67.6 0.2 reshape.19
  67.8 40.1 %all_to_all.17 = bf16[32,4,2560]{2,1,0:T(4,128)(2,1)S(1)} all-to-all(bf16[32,4,2560]{2,1,0:T(4,128)(2,1)S(1)} %reshape.19), channel_id=1, replica_groups=mesh['section'=24,'y'=8,'zh'=4] {'y','zh'}, dimensions={0} | all-to-all | bytes 1310720 | tf_op jit(solution)/shard_map/all_to_all | solution.py:43
  107.9 0.3 reduce_sum.12
  108.2 3.0 %collective-permute-start = (bf16[4,2560]{1,0:T(4,128)(2,1)S(1)}, bf16[4,2560]{1,0:T(4,128)(2,1)S(1)}, u32[]{:S(2)}, u32[]{:S(2)}) collective-permute-start(bf16[4,2560]{1,0:T(4,128)(2,1)S(1)} %reduce_sum.12), channel_id=1, source_target_pairs={{32,0},{64,32},{96,64},{128,96},{160,128},{192,160},{224,192},{256... | collective-permute-start | bytes 61448 | tf_op jit(solution)/shard_map/ppermute | solution.py:12
  111.2 4.2 %collective-permute-done = bf16[4,2560]{1,0:T(4,128)(2,1)S(1)} collective-permute-done((bf16[4,2560]{1,0:T(4,128)(2,1)S(1)}, bf16[4,2560]{1,0:T(4,128)(2,1)S(1)}, u32[]{:S(2)}, u32[]{:S(2)}) %collective-permute-start) | collective-permute-done | bytes 20512 | tf_op jit(solution)/shard_map/ppermute | solution.py:12
  115.4 0.6 copy.10
  (2 shorter events, 0.1 us)
Async XLA Ops:
  0.0 61.2 %copy-start = (bf16[2560,432]{0,1:T(8,128)(2,1)S(1)}, bf16[2560,432]{0,1:T(8,128)(2,1)}, u32[]{:S(2)}) copy-start(bf16[2560,432]{0,1:T(8,128)(2,1)} %param.8) | copy-start | bytes 6635524
  24.3 34.6 %copy-start.2 = (bf16[432,2560]{1,0:T(8,128)(2,1)S(1)}, bf16[432,2560]{1,0:T(8,128)(2,1)}, u32[]{:S(2)}) copy-start(bf16[432,2560]{1,0:T(8,128)(2,1)} %param.9) | copy-start | bytes 6635524
  58.8 1.6 %copy-start.1 = (bf16[2560,432]{0,1:T(8,128)(2,1)S(1)}, bf16[2560,432]{0,1:T(8,128)(2,1)}, u32[]{:S(2)}) copy-start(bf16[2560,432]{0,1:T(8,128)(2,1)} %param.7) | copy-start | bytes 6635524
  108.2 7.2 %collective-permute-start = (bf16[4,2560]{1,0:T(4,128)(2,1)S(1)}, bf16[4,2560]{1,0:T(4,128)(2,1)S(1)}, u32[]{:S(2)}, u32[]{:S(2)}) collective-permute-start(bf16[4,2560]{1,0:T(4,128)(2,1)S(1)} %reduce_sum.12), channel_id=1, source_target_pairs={{32,0},{64,32},{96,64},{128,96},{160,128},{192,160},{224,192},{256... | collective-permute-start | bytes 61448 | tf_op jit(solution)/shard_map/ppermute | solution.py:12

commit v2 on v1

v2 whole, which is shorter than its diff:
```python
import jax
import jax.numpy as jnp
from jax import lax
from jax.experimental import pallas as pl
from jax.experimental.pallas import tpu as pltpu
from jax.sharding import Mesh, PartitionSpec as P

TP = ("y", "zh")


def passed_along(block, axis, distance):
    devices = range(lax.axis_size(axis))
    route = [(i - distance, i) for i in devices if i - distance in devices]
    return lax.ppermute(block, axis, route)


def layer_kernel(far_ref, w_gate_ref, w_up_ref, w_down_hbm, out_ref, w_down_ref, arrived):
    fetch = pltpu.make_async_copy(w_down_hbm, w_down_ref, arrived)
    fetch.start()
    ny, both, width = far_ref.shape
    rows = both // 2
    nt = (((1,), (1,)), ((), ()))
    nn = (((1,), (0,)), ((), ()))
    x = far_ref[:, :rows, :].reshape(ny * rows, width)
    g = far_ref[:, rows:, :].reshape(ny * rows, width)
    gate = lax.dot_general(x, w_gate_ref[...], nt, preferred_element_type=jnp.float32)
    up = lax.dot_general(x, w_up_ref[...], nt, preferred_element_type=jnp.float32)
    fetch.wait()
    hid_grad = lax.dot_general(g, w_down_ref[...], nt, preferred_element_type=jnp.float32)
    sig = jax.nn.sigmoid(gate)
    hid_sig = hid_grad * sig
    up_grad = (hid_sig * gate).astype(jnp.bfloat16)
    gate_grad = (hid_sig * up * (1.0 + gate * (1.0 - sig))).astype(jnp.bfloat16)
    total = lax.dot_general(gate_grad, w_gate_ref[...], nn, preferred_element_type=jnp.float32)
    total = total + lax.dot_general(up_grad, w_up_ref[...], nn, preferred_element_type=jnp.float32)
    out_ref[...] = total.astype(jnp.bfloat16)


def hidden_and_back(far, w_gate, w_up, w_down):
    ny, both, width = far.shape
    hidden = w_gate.shape[0]
    tokens = ny * both // 2
    whole = pl.BlockSpec(memory_space=pltpu.VMEM)
    return pl.pallas_call(
        layer_kernel,
        out_shape=jax.ShapeDtypeStruct((tokens, width), jnp.bfloat16),
        in_specs=[whole] * 3 + [pl.BlockSpec(memory_space=pl.ANY)],
        out_specs=whole,
        scratch_shapes=[pltpu.VMEM(w_down.shape, w_down.dtype), pltpu.SemaphoreType.DMA],
        compiler_params=pltpu.CompilerParams(vmem_limit_bytes=16 * 2**20),
        cost_estimate=pl.CostEstimate(
            flops=10 * tokens * width * hidden,
            bytes_accessed=2 * (far.size + 3 * hidden * width + tokens * width),
            transcendentals=tokens * hidden,
        ),
    )(far, w_gate, w_up, w_down)


def on_device(inputs, out_grad, w_gate, w_up, w_down):
    rows, width = inputs.shape[1:]
    ny, nz = lax.axis_size("y"), lax.axis_size("zh")
    both = jnp.concatenate([inputs[0], out_grad[0]], axis=0)
    near = lax.all_to_all(
        jnp.broadcast_to(both, (nz,) + both.shape), "zh", 0, 0, tiled=True
    )
    near = near.reshape(nz, 2, rows, width).transpose(1, 0, 2, 3)
    near = near.reshape(2 * nz * rows, width)
    far = lax.all_to_all(
        jnp.broadcast_to(near, (ny,) + near.shape), "y", 0, 0, tiled=True
    )
    total = hidden_and_back(far, w_gate.T, w_up.T, w_down)
    parts = total.reshape(ny * nz, rows, width)
    parts = lax.all_to_all(parts, TP, 0, 0, tiled=True)
    in_grad = jnp.sum(parts.astype(jnp.float32), axis=0).astype(jnp.bfloat16)
    return passed_along(in_grad, "section", -1)[None]


def solution(mesh):
    n_section, n_tp = mesh.devices.shape
    fine = Mesh(mesh.devices.reshape(n_section, 8, n_tp // 8), ("section",) + TP)
    placed = (
        P("section", TP, None),
        P("section", TP, None),
        P(None, TP),
        P(None, TP),
        P(TP, None),
    )
    return jax.shard_map(
        on_device, mesh=fine, in_specs=placed, out_specs=P("section", TP, None), check_vma=False
    )
```

time: 116 us -> 113 us (0.974)
  matrix products: 7.87 us -> 0 us
  Pallas kernels: 0 us -> 3.82 us
    dot_general x4 -> x0, matrix products: 7.87 us -> none  [the longest x1 4.54 us: on_device(): lax.dot_general(gate_grad, w_gate, (((1,), (1,)), ((), ())), preferred_el...]
    pallas_call x0 -> x1, Pallas kernels: none -> 3.82 us  [hidden_and_back(): pl.pallas_call(layer_kernel, out_shape=jax.ShapeDtypeStruct((tokens, widt...]
where the time goes in v2:
time: 113 us
  blocking collectives  97.8 us (87%)
  waiting for transfers between devices  4.16 us (4%)
  Pallas kernels  3.82 us (3%)
  starting transfers between devices  3.04 us (3%)
  local copies, waits for them, and re-layouts  2.7 us (2%)
    all_to_all x1, blocking collectives, on_device(): parts = lax.all_to_all(parts, TP, 0, 0, tiled=True)  40.1 us
    all_to_all x1, blocking collectives, on_device(): lax.all_to_all(jnp.broadcast_to(near, (ny,) + near.shape), 'y', 0, 0, til...  34.6 us
    all_to_all x1, blocking collectives, on_device(): lax.all_to_all(jnp.broadcast_to(both, (nz,) + both.shape), 'zh', 0, 0, ti...  23 us
    ppermute x1, waiting for transfers between devices, passed_along(): return lax.ppermute(block, axis, route)  4.16 us
    pallas_call x1, Pallas kernels, hidden_and_back(): pl.pallas_call(layer_kernel, out_shape=jax.ShapeDtypeStruct((tokens, widt...  3.82 us
    ppermute x1, starting transfers between devices, passed_along(): return lax.ppermute(block, axis, route)  3.04 us
  transfers between devices with their start and end apart: 1, of which 1 were waited for; matrix products, arithmetic and copies ran while one was open for 0% of the time, Pallas kernels for 0%

profile of v2, /device:TPU:79, one launch (start us, length us, event | category | flops | bytes accessed | tf_op | source)
XLA Modules:
  0.0 112.6 jit_solution(15227172145177005903)
XLA Ops:
  0.0 0.8 pad_maximum_fusion
  0.8 23.0 %all_to_all.15 = bf16[4,8,2560]{2,1,0:T(8,128)(2,1)S(1)} all-to-all(bf16[4,8,2560]{2,1,0:T(8,128)(2,1)S(1)} %broadcast_in_dim.9), channel_id=1, replica_groups=mesh['section'=24,'y'=8,'zh'=4] {'zh'}, dimensions={0} | all-to-all | bytes 327680 | tf_op jit(solution)/shard_map/all_to_all | solution.py:63
  23.8 0.1 copy.7
  23.9 0.1 copy.8
  24.0 0.0 copy-start
  24.1 0.0 copy-start.1
  24.1 0.1 broadcast_in_dim.10
  24.2 34.6 %all_to_all.16.far_ref = bf16[8,32,2560]{2,1,0:T(8,128)(2,1)S(1)} all-to-all(bf16[8,32,2560]{2,1,0:T(8,128)(2,1)S(1)} %broadcast_in_dim.10), channel_id=1, replica_groups=mesh['section'=24,'y'=8,'zh'=4] {'y'}, dimensions={0} | all-to-all | bytes 2621440 | tf_op jit(solution)/shard_map/all_to_all | solution.py:68
  58.8 0.0 copy-done
  58.8 0.0 copy-done.1
  58.8 0.0 copy-start.2
  58.8 1.6 %copy-done.2 = bf16[432,2560]{1,0:T(8,128)(2,1)S(1)} copy-done((bf16[432,2560]{1,0:T(8,128)(2,1)S(1)}, bf16[432,2560]{1,0:T(8,128)(2,1)}, u32[]{:S(2)}) %copy-start.2) | copy-done | bytes 2211864
  60.5 3.8 %shard_map.55 = bf16[128,2560]{1,0:T(8,128)(2,1)S(1)} custom-call(bf16[8,32,2560]{2,1,0:T(8,128)(2,1)S(1)} %all_to_all.16.far_ref, bf16[432,2560]{1,0:T(8,128)(2,1)S(1)} %bitcast.8, bf16[432,2560]{1,0:T(8,128)(2,1)S(1)} %bitcast.9, bf16[432,2560]{1,0:T(8,128)(2,1)S(1)} %copy-done.2), custom_call_target="tpu_custom_call" | custom-call | flops 1415577600 | bytes 8601600 | tf_op jit(solution)/shard_map/pallas_call | solution.py:44
  64.3 0.2 reshape.11
  64.4 40.1 %all_to_all.17 = bf16[32,4,2560]{2,1,0:T(4,128)(2,1)S(1)} all-to-all(bf16[32,4,2560]{2,1,0:T(4,128)(2,1)S(1)} %reshape.11), channel_id=1, replica_groups=mesh['section'=24,'y'=8,'zh'=4] {'y','zh'}, dimensions={0} | all-to-all | bytes 1310720 | tf_op jit(solution)/shard_map/all_to_all | solution.py:73
  104.5 0.3 reduce_sum.12
  104.8 3.0 %collective-permute-start = (bf16[4,2560]{1,0:T(4,128)(2,1)S(1)}, bf16[4,2560]{1,0:T(4,128)(2,1)S(1)}, u32[]{:S(2)}, u32[]{:S(2)}) collective-permute-start(bf16[4,2560]{1,0:T(4,128)(2,1)S(1)} %reduce_sum.12), channel_id=1, source_target_pairs={{32,0},{64,32},{96,64},{128,96},{160,128},{192,160},{224,192},{256... | collective-permute-start | bytes 61448 | tf_op jit(solution)/shard_map/ppermute | solution.py:14
  107.9 4.2 %collective-permute-done = bf16[4,2560]{1,0:T(4,128)(2,1)S(1)} collective-permute-done((bf16[4,2560]{1,0:T(4,128)(2,1)S(1)}, bf16[4,2560]{1,0:T(4,128)(2,1)S(1)}, u32[]{:S(2)}, u32[]{:S(2)}) %collective-permute-start) | collective-permute-done | bytes 20512 | tf_op jit(solution)/shard_map/ppermute | solution.py:14
  112.0 0.6 copy.10
  (2 shorter events, 0.1 us)
Async XLA Ops:
  24.0 34.8 %copy-start = (bf16[2560,432]{0,1:T(8,128)(2,1)S(1)}, bf16[2560,432]{0,1:T(8,128)(2,1)}, u32[]{:S(2)}) copy-start(bf16[2560,432]{0,1:T(8,128)(2,1)} %param.7) | copy-start | bytes 6635524
  24.1 34.8 %copy-start.1 = (bf16[2560,432]{0,1:T(8,128)(2,1)S(1)}, bf16[2560,432]{0,1:T(8,128)(2,1)}, u32[]{:S(2)}) copy-start(bf16[2560,432]{0,1:T(8,128)(2,1)} %param.8) | copy-start | bytes 6635524
  58.8 1.6 %copy-start.2 = (bf16[432,2560]{1,0:T(8,128)(2,1)S(1)}, bf16[432,2560]{1,0:T(8,128)(2,1)}, u32[]{:S(2)}) copy-start(bf16[432,2560]{1,0:T(8,128)(2,1)} %w_down_hbm.1) | copy-start | bytes 6635524
  104.8 7.2 %collective-permute-start = (bf16[4,2560]{1,0:T(4,128)(2,1)S(1)}, bf16[4,2560]{1,0:T(4,128)(2,1)S(1)}, u32[]{:S(2)}, u32[]{:S(2)}) collective-permute-start(bf16[4,2560]{1,0:T(4,128)(2,1)S(1)} %reduce_sum.12), channel_id=1, source_target_pairs={{32,0},{64,32},{96,64},{128,96},{160,128},{192,160},{224,192},{256... | collective-permute-start | bytes 61448 | tf_op jit(solution)/shard_map/ppermute | solution.py:14

commit v3 on v2

v3 whole, which is shorter than its diff:
```python
import jax
import jax.numpy as jnp
from jax import lax
from jax.experimental import pallas as pl
from jax.experimental.pallas import tpu as pltpu
from jax.sharding import Mesh, PartitionSpec as P

TP = ("half", "odd", "zh")
JOINT = True


def handed_on(block, across, back):
    n, ny = lax.axis_size("section"), lax.axis_size("half") * lax.axis_size("odd")
    route = [
        (s * ny + y, (s - back) * ny + (y + (1 - 2 * ((y + s) % 2)) * across) % ny)
        for s in range(back, n)
        for y in range(ny)
    ]
    return lax.ppermute(block, ("section", "half", "odd"), route)


def layer_kernel(far_ref, w_gate_ref, w_up_ref, w_down_ref, out_ref):
    n, both, width = far_ref.shape
    rows = both // 2
    nt = (((1,), (1,)), ((), ()))
    nn = (((1,), (0,)), ((), ()))
    x = far_ref[:, :rows, :].reshape(n * rows, width)
    g = far_ref[:, rows:, :].reshape(n * rows, width)
    gate = lax.dot_general(x, w_gate_ref[...], nt, preferred_element_type=jnp.float32)
    up = lax.dot_general(x, w_up_ref[...], nt, preferred_element_type=jnp.float32)
    hid_grad = lax.dot_general(g, w_down_ref[...], nt, preferred_element_type=jnp.float32)
    sig = jax.nn.sigmoid(gate)
    hid_sig = hid_grad * sig
    up_grad = (hid_sig * gate).astype(jnp.bfloat16)
    gate_grad = (hid_sig * up * (1.0 + gate * (1.0 - sig))).astype(jnp.bfloat16)
    total = lax.dot_general(gate_grad, w_gate_ref[...], nn, preferred_element_type=jnp.float32)
    total = total + lax.dot_general(up_grad, w_up_ref[...], nn, preferred_element_type=jnp.float32)
    out_ref[...] = total.astype(out_ref.dtype)


def layer(far, w_gate, w_up, w_down, kind):
    n, both, width = far.shape
    hidden = w_gate.shape[0]
    tokens = n * both // 2
    whole = pl.BlockSpec(memory_space=pltpu.VMEM)
    return pl.pallas_call(
        layer_kernel,
        out_shape=jax.ShapeDtypeStruct((tokens, width), kind),
        in_specs=[whole] * 4,
        out_specs=whole,
        compiler_params=pltpu.CompilerParams(vmem_limit_bytes=16 * 2**20),
        cost_estimate=pl.CostEstimate(
            flops=10 * tokens * width * hidden,
            bytes_accessed=2 * (far.size + 3 * hidden * width + tokens * width),
            transcendentals=tokens * hidden,
        ),
    )(far, w_gate, w_up, w_down)


def on_device(inputs, out_grad, w_gate, w_up, w_down):
    rows, width = inputs.shape[1:]
    nh, nz = lax.axis_size("half"), lax.axis_size("zh")
    both = jnp.concatenate([inputs[0], out_grad[0]], axis=0)
    if JOINT:
        near = lax.all_to_all(
            jnp.broadcast_to(both, (nh * nz,) + both.shape), ("half", "zh"), 0, 0, tiled=True
        )
        own = near.reshape(nh, nz, 2, rows, width).transpose(0, 2, 1, 3, 4)
        own = own.reshape(nh, 2 * nz * rows, width)
    else:
        near = lax.all_to_all(
            jnp.broadcast_to(both, (nz,) + both.shape), "zh", 0, 0, tiled=True
        )
        near = near.reshape(nz, 2, rows, width).transpose(1, 0, 2, 3)
        near = near.reshape(2 * nz * rows, width)
        own = lax.all_to_all(
            jnp.broadcast_to(near, (nh,) + near.shape), "half", 0, 0, tiled=True
        )
    weights = (w_gate.T, w_up.T, w_down)
    other = handed_on(own, 1, 0)
    kept = layer(own, *weights, jnp.bfloat16)
    other, kept = lax.optimization_barrier((other, kept))
    kept = handed_on(kept, 0, 1)
    lent = layer(other, *weights, jnp.bfloat16)
    lent = handed_on(lent, 1, 1)
    total = kept.astype(jnp.float32) + lent.astype(jnp.float32)
    parts = total.astype(jnp.bfloat16).reshape(nh * nz, rows, width)
    parts = lax.all_to_all(parts, ("half", "zh"), 0, 0, tiled=True)
    in_grad = jnp.sum(parts.astype(jnp.float32), axis=0).astype(jnp.bfloat16)
    return in_grad[None]


def solution(mesh):
    n_section, n_tp = mesh.devices.shape
    fine = Mesh(mesh.devices.reshape(n_section, 4, 2, n_tp // 8), ("section",) + TP)
    placed = (
        P("section", TP, None),
        P("section", TP, None),
        P(None, TP),
        P(None, TP),
        P(TP, None),
    )
    return jax.shard_map(
        on_device, mesh=fine, in_specs=placed, out_specs=P("section", TP, None), check_vma=False
    )
```

time: 113 us -> 105 us (0.929)
  the two profiles are of different devices: /device:TPU:79 before, /device:TPU:67 now
where the time goes in v3:
time: 105 us
  blocking collectives  73.6 us (70%)
  waiting for transfers between devices  10.8 us (10%)
  starting transfers between devices  8.32 us (8%)
  Pallas kernels  6.52 us (6%)
  local copies, waits for them, and re-layouts  3.92 us (4%)
  other arithmetic  1.6 us (2%)
    all_to_all x1, blocking collectives, on_device(): lax.all_to_all(jnp.broadcast_to(both, (nh * nz,) + both.shape), ('half',...  50.6 us
    all_to_all x1, blocking collectives, on_device(): parts = lax.all_to_all(parts, ('half', 'zh'), 0, 0, tiled=True)  23 us
    ppermute x3, waiting for transfers between devices, handed_on(): return lax.ppermute(block, ('section', 'half', 'odd'), route)  10.8 us
    ppermute x3, starting transfers between devices, handed_on(): return lax.ppermute(block, ('section', 'half', 'odd'), route)  8.32 us
    pallas_call x2, Pallas kernels, layer(): pl.pallas_call(layer_kernel, out_shape=jax.ShapeDtypeStruct((tokens, widt...  6.52 us
    unnamed x8, local copies, waits for them, and re-layouts  3.25 us
  transfers between devices with their start and end apart: 3, of which 3 were waited for; matrix products, arithmetic and copies ran while one was open for 0% of the time, Pallas kernels for 3%

profile of v3, /device:TPU:67, one launch (start us, length us, event | category | flops | bytes accessed | tf_op | source)
XLA Modules:
  0.0 104.9 jit_solution(17731357148442275708)
XLA Ops:
  0.0 0.8 pad_maximum_fusion
  0.8 50.6 %all_to_all.10 = bf16[16,8,2560]{2,1,0:T(8,128)(2,1)S(1)} all-to-all(bf16[16,8,2560]{2,1,0:T(8,128)(2,1)S(1)} %broadcast_in_dim.6), channel_id=1, replica_groups=mesh['section'=24,'half'=4,'odd'=2,'zh'=4] {'half','zh'}, dimensions={0} | all-to-all | bytes 1310720 | tf_op jit(solution)/shard_map/all_to_all | solution.py:65
  51.5 0.0 copy-start
  51.5 0.1 reshape.9
  51.6 0.2 copy.6
  51.9 0.1 reshape.10.far_ref
  52.0 2.8 %collective-permute-start = (bf16[4,32,2560]{2,1,0:T(8,128)(2,1)S(1)}, bf16[4,32,2560]{2,1,0:T(8,128)(2,1)S(1)}, u32[]{:S(2)}, u32[]{:S(2)}) collective-permute-start(bf16[4,32,2560]{2,1,0:T(8,128)(2,1)S(1)} %reshape.10.far_ref), channel_id=1, source_target_pairs={{0,4},{4,0},{8,12},{12,8},{16,20},{20,16},{24,28},{28,24},{32,60},... | collective-permute-start | bytes 1966088 | tf_op jit(solution)/shard_map/ppermute | solution.py:19
  54.8 0.0 copy-done
  54.8 0.0 copy-start.1
  54.8 1.6 %copy-done.1 = bf16[2560,432]{0,1:T(8,128)(2,1)S(1)} copy-done((bf16[2560,432]{0,1:T(8,128)(2,1)S(1)}, bf16[2560,432]{0,1:T(8,128)(2,1)}, u32[]{:S(2)}) %copy-start.1) | copy-done | bytes 2211864
  56.5 0.0 copy-start.3
  56.5 1.6 %copy-done.3 = bf16[432,2560]{1,0:T(8,128)(2,1)S(1)} copy-done((bf16[432,2560]{1,0:T(8,128)(2,1)S(1)}, bf16[432,2560]{1,0:T(8,128)(2,1)}, u32[]{:S(2)}) %copy-start.3) | copy-done | bytes 2211864
  58.1 3.3 %shard_map.55 = bf16[64,2560]{1,0:T(8,128)(2,1)S(1)} custom-call(bf16[4,32,2560]{2,1,0:T(8,128)(2,1)S(1)} %reshape.10.far_ref, bf16[432,2560]{1,0:T(8,128)(2,1)S(1)} %bitcast.6, bf16[432,2560]{1,0:T(8,128)(2,1)S(1)} %bitcast.8, bf16[432,2560]{1,0:T(8,128)(2,1)S(1)} %copy-done.3), custom_call_target="tpu_custom_call" | custom-call | flops 707788800 | bytes 7618560 | tf_op jit(solution)/shard_map/pallas_call | solution.py:46
  61.3 3.4 %collective-permute-done.far_ref = bf16[4,32,2560]{2,1,0:T(8,128)(2,1)S(1)} collective-permute-done((bf16[4,32,2560]{2,1,0:T(8,128)(2,1)S(1)}, bf16[4,32,2560]{2,1,0:T(8,128)(2,1)S(1)}, u32[]{:S(2)}, u32[]{:S(2)}) %collective-permute-start) | collective-permute-done | bytes 655392 | tf_op jit(solution)/shard_map/ppermute | solution.py:19
  64.7 0.0 copy-done.2
  64.7 3.3 %shard_map.56 = bf16[64,2560]{1,0:T(8,128)(2,1)S(1)} custom-call(bf16[4,32,2560]{2,1,0:T(8,128)(2,1)S(1)} %collective-permute-done.far_ref, bf16[432,2560]{1,0:T(8,128)(2,1)S(1)} %bitcast.7, bf16[432,2560]{1,0:T(8,128)(2,1)S(1)} %bitcast.9, bf16[432,2560]{1,0:T(8,128)(2,1)S(1)} %copy-done.3), custom_call_target="tpu_custom_call" | custom-call | flops 707788800 | bytes 7618560 | tf_op jit(solution)/shard_map/pallas_call | solution.py:46
  68.0 3.6 %collective-permute-start.2 = (bf16[64,2560]{1,0:T(8,128)(2,1)S(1)}, bf16[64,2560]{1,0:T(8,128)(2,1)S(1)}, u32[]{:S(2)}, u32[]{:S(2)}) collective-permute-start(bf16[64,2560]{1,0:T(8,128)(2,1)S(1)} %shard_map.56), channel_id=1, source_target_pairs={{32,28},{36,8},{40,4},{44,16},{48,12},{52,24},{56,20},{60,0},{64,3... | collective-permute-start | bytes 983048 | tf_op jit(solution)/shard_map/ppermute | solution.py:19
  71.6 1.9 %collective-permute-start.1 = (bf16[64,2560]{1,0:T(8,128)(2,1)S(1)}, bf16[64,2560]{1,0:T(8,128)(2,1)S(1)}, u32[]{:S(2)}, u32[]{:S(2)}) collective-permute-start(bf16[64,2560]{1,0:T(8,128)(2,1)S(1)} %shard_map.55), channel_id=1, source_target_pairs={{32,0},{36,4},{40,8},{44,12},{48,16},{52,20},{56,24},{60,28},{64,3... | collective-permute-start | bytes 983048 | tf_op jit(solution)/shard_map/ppermute | solution.py:19
  73.5 4.2 %collective-permute-done.2 = bf16[64,2560]{1,0:T(8,128)(2,1)S(1)} collective-permute-done((bf16[64,2560]{1,0:T(8,128)(2,1)S(1)}, bf16[64,2560]{1,0:T(8,128)(2,1)S(1)}, u32[]{:S(2)}, u32[]{:S(2)}) %collective-permute-start.2) | collective-permute-done | bytes 327712 | tf_op jit(solution)/shard_map/ppermute | solution.py:19
  77.8 3.2 %collective-permute-done.1 = bf16[64,2560]{1,0:T(8,128)(2,1)S(1)} collective-permute-done((bf16[64,2560]{1,0:T(8,128)(2,1)S(1)}, bf16[64,2560]{1,0:T(8,128)(2,1)S(1)}, u32[]{:S(2)}, u32[]{:S(2)}) %collective-permute-start.1) | collective-permute-done | bytes 327712 | tf_op jit(solution)/shard_map/ppermute | solution.py:19
  81.0 0.1 add_convert_fusion
  81.1 0.1 reshape.11
  81.2 23.0 %all_to_all.11 = bf16[16,4,2560]{2,1,0:T(4,128)(2,1)S(1)} all-to-all(bf16[16,4,2560]{2,1,0:T(4,128)(2,1)S(1)} %reshape.11), channel_id=1, replica_groups=mesh['section'=24,'half'=4,'odd'=2,'zh'=4] {'half','zh'}, dimensions={0} | all-to-all | bytes 655360 | tf_op jit(solution)/shard_map/all_to_all | solution.py:88
  104.1 0.8 reduce_sum.12
  (2 shorter events, 0.0 us)
Async XLA Ops:
  51.5 3.4 %copy-start = (bf16[2560,432]{0,1:T(8,128)(2,1)S(1)}, bf16[2560,432]{0,1:T(8,128)(2,1)}, u32[]{:S(2)}) copy-start(bf16[2560,432]{0,1:T(8,128)(2,1)} %param.7) | copy-start | bytes 6635524
  52.0 12.7 %collective-permute-start = (bf16[4,32,2560]{2,1,0:T(8,128)(2,1)S(1)}, bf16[4,32,2560]{2,1,0:T(8,128)(2,1)S(1)}, u32[]{:S(2)}, u32[]{:S(2)}) collective-permute-start(bf16[4,32,2560]{2,1,0:T(8,128)(2,1)S(1)} %reshape.10.far_ref), channel_id=1, source_target_pairs={{0,4},{4,0},{8,12},{12,8},{16,20},{20,16},{24,28},{28,24},{32,60},... | collective-permute-start | bytes 1966088 | tf_op jit(solution)/shard_map/ppermute | solution.py:19
  54.8 1.6 %copy-start.1 = (bf16[2560,432]{0,1:T(8,128)(2,1)S(1)}, bf16[2560,432]{0,1:T(8,128)(2,1)}, u32[]{:S(2)}) copy-start(bf16[2560,432]{0,1:T(8,128)(2,1)} %param.8) | copy-start | bytes 6635524
  56.5 1.6 %copy-start.3 = (bf16[432,2560]{1,0:T(8,128)(2,1)S(1)}, bf16[432,2560]{1,0:T(8,128)(2,1)}, u32[]{:S(2)}) copy-start(bf16[432,2560]{1,0:T(8,128)(2,1)} %w_down_ref.3) | copy-start | bytes 6635524
  58.1 6.6 %copy-start.2 = (bf16[2560,432]{0,1:T(8,128)(2,1)S(1)}, bf16[2560,432]{0,1:T(8,128)(2,1)}, u32[]{:S(2)}) copy-start(bf16[2560,432]{0,1:T(8,128)(2,1)} %param.8) | copy-start | bytes 6635524
  68.0 9.8 %collective-permute-start.2 = (bf16[64,2560]{1,0:T(8,128)(2,1)S(1)}, bf16[64,2560]{1,0:T(8,128)(2,1)S(1)}, u32[]{:S(2)}, u32[]{:S(2)}) collective-permute-start(bf16[64,2560]{1,0:T(8,128)(2,1)S(1)} %shard_map.56), channel_id=1, source_target_pairs={{32,28},{36,8},{40,4},{44,16},{48,12},{52,24},{56,20},{60,0},{64,3... | collective-permute-start | bytes 983048 | tf_op jit(solution)/shard_map/ppermute | solution.py:19
  71.6 9.4 %collective-permute-start.1 = (bf16[64,2560]{1,0:T(8,128)(2,1)S(1)}, bf16[64,2560]{1,0:T(8,128)(2,1)S(1)}, u32[]{:S(2)}, u32[]{:S(2)}) collective-permute-start(bf16[64,2560]{1,0:T(8,128)(2,1)S(1)} %shard_map.55), channel_id=1, source_target_pairs={{32,0},{36,4},{40,8},{44,12},{48,16},{52,20},{56,24},{60,28},{64,3... | collective-permute-start | bytes 983048 | tf_op jit(solution)/shard_map/ppermute | solution.py:19

commit v4 on v1

v4 whole, which is shorter than its diff:
```python
import jax
import jax.numpy as jnp
from jax import lax
from jax.experimental import pallas as pl
from jax.experimental.pallas import tpu as pltpu
from jax.sharding import Mesh, PartitionSpec as P

TP = ("half", "odd", "zh")
NT = (((1,), (1,)), ((), ()))
NN = (((1,), (0,)), ((), ()))
VMEM = pl.BlockSpec(memory_space=pltpu.VMEM)
PARAMS = pltpu.CompilerParams(vmem_limit_bytes=16 * 2**20)


def handed_on(block, across, back):
    n, ny = lax.axis_size("section"), lax.axis_size("half") * lax.axis_size("odd")
    route = [
        (s * ny + y, (s - back) * ny + (y + (1 - 2 * ((y + s) % 2)) * across) % ny)
        for s in range(back, n)
        for y in range(ny)
    ]
    return lax.ppermute(block, ("section", "half", "odd"), route)


def dot(a, b, dims):
    return lax.dot_general(a, b, dims, preferred_element_type=jnp.float32)


def sorted_rows(near_ref):
    n, eight, width = near_ref.shape
    pairs = near_ref[...].astype(jnp.float32).reshape(n // 2, 2, eight, width)
    even, odd = pairs[:, 0], pairs[:, 1]
    upper = lax.broadcasted_iota(jnp.int32, even.shape, 1) < eight // 2
    x = jnp.where(upper, even, pltpu.roll(odd, eight // 2, 1))
    g = jnp.where(upper, pltpu.roll(even, eight // 2, 1), odd)
    return [r.reshape(n * eight // 2, width).astype(near_ref.dtype) for r in (x, g)]


def gate_factors(gate, up):
    sig = jax.nn.sigmoid(gate)
    return up * sig * (1.0 + gate * (1.0 - sig)), gate * sig


def back(g, for_gate, for_up, w_gate, w_up, w_down):
    hid_grad = dot(g, w_down, NT)
    gate_grad = (hid_grad * for_gate).astype(jnp.bfloat16)
    up_grad = (hid_grad * for_up).astype(jnp.bfloat16)
    return dot(gate_grad, w_gate, NN) + dot(up_grad, w_up, NN)


def first_kernel(
    near_ref, w_gate_ref, w_up_hbm, w_down_hbm, out_ref, w_up_ref, w_down_ref, up_here, down_here
):
    up = pltpu.make_async_copy(w_up_hbm, w_up_ref, up_here)
    down = pltpu.make_async_copy(w_down_hbm, w_down_ref, down_here)
    up.start()
    down.start()
    x, g = sorted_rows(near_ref)
    gate = dot(x, w_gate_ref[...], NT)
    up.wait()
    factors = gate_factors(gate, dot(x, w_up_ref[...], NT))
    down.wait()
    total = back(g, *factors, w_gate_ref[...], w_up_ref[...], w_down_ref[...])
    out_ref[...] = total.astype(out_ref.dtype)


def cost(near, w_down):
    tokens = near.size // (2 * near.shape[-1])
    return pl.CostEstimate(
        flops=10 * tokens * w_down.size,
        bytes_accessed=6 * w_down.size + 2 * near.size,
        transcendentals=tokens * w_down.shape[0],
    )


def first(near, w_gate, w_up, w_down):
    tokens, width = near.size // (2 * near.shape[-1]), near.shape[-1]
    return pl.pallas_call(
        first_kernel,
        out_shape=[
            jax.ShapeDtypeStruct((tokens, width), near.dtype),
            jax.ShapeDtypeStruct(w_up.shape, w_up.dtype),
            jax.ShapeDtypeStruct(w_down.shape, w_down.dtype),
        ],
        in_specs=[VMEM] * 2 + [pl.BlockSpec(memory_space=pltpu.HBM)] * 2,
        out_specs=[VMEM] * 3,
        scratch_shapes=[pltpu.SemaphoreType.DMA] * 2,
        compiler_params=PARAMS,
        cost_estimate=cost(near, w_down),
    )(near, w_gate, *(pltpu.with_memory_space_constraint(w, pltpu.HBM) for w in (w_up, w_down)))


def second_kernel(near_ref, w_gate_ref, w_up_ref, w_down_ref, token_ref, out_ref):
    x, g = sorted_rows(near_ref)
    factors = gate_factors(dot(x, w_gate_ref[...], NT), dot(x, w_up_ref[...], NT))
    total = back(g, *factors, w_gate_ref[...], w_up_ref[...], w_down_ref[...])
    out_ref[...] = total.astype(out_ref.dtype)


def second(near, *operands):
    tokens, width = near.size // (2 * near.shape[-1]), near.shape[-1]
    return pl.pallas_call(
        second_kernel,
        out_shape=jax.ShapeDtypeStruct((tokens, width), near.dtype),
        in_specs=[VMEM] * (1 + len(operands)),
        out_specs=VMEM,
        compiler_params=PARAMS,
        cost_estimate=cost(near, operands[2]),
    )(near, *operands)


def turn_kernel(kept_ref, token_ref):
    token_ref[...] = kept_ref[: token_ref.shape[0], : token_ref.shape[1]].astype(token_ref.dtype)


def turn(kept):
    return pl.pallas_call(
        turn_kernel,
        out_shape=jax.ShapeDtypeStruct((8, 128), jnp.float32),
        in_specs=[VMEM],
        out_specs=VMEM,
        compiler_params=PARAMS,
    )(kept)


def on_device(inputs, out_grad, w_gate, w_up, w_down):
    rows, width = inputs.shape[1:]
    nh, nz = lax.axis_size("half"), lax.axis_size("zh")
    both = jnp.concatenate([inputs[0], out_grad[0]], axis=0)
    w_gate, w_up = w_gate.T, w_up.T
    near = lax.all_to_all(
        jnp.broadcast_to(both, (nh * nz,) + both.shape), ("half", "zh"), 0, 0, tiled=True
    )
    other = handed_on(near, 1, 0)
    kept, w_up, w_down = first(near, w_gate, w_up, w_down)
    sent = handed_on(kept, 0, 1)
    token = turn(kept)
    lent = second(other, w_gate, w_up, w_down, token)
    lent = handed_on(lent, 1, 1)
    total = sent.astype(jnp.float32) + lent.astype(jnp.float32)
    parts = total.astype(jnp.bfloat16).reshape(nh * nz, rows, width)
    parts = lax.all_to_all(parts, ("half", "zh"), 0, 0, tiled=True)
    in_grad = jnp.sum(parts.astype(jnp.float32), axis=0).astype(jnp.bfloat16)
    return in_grad[None]


def solution(mesh):
    n_section, n_tp = mesh.devices.shape
    fine = Mesh(mesh.devices.reshape(n_section, 4, 2, n_tp // 8), ("section",) + TP)
    placed = (
        P("section", TP, None),
        P("section", TP, None),
        P(None, TP),
        P(None, TP),
        P(TP, None),
    )
    return jax.shard_map(
        on_device, mesh=fine, in_specs=placed, out_specs=P("section", TP, None), check_vma=False
    )
```

time: 116 us -> 102 us (0.88)
  the two profiles are of different devices: /device:TPU:79 before, /device:TPU:71 now
where the time goes in v4:
time: 102 us; the launch traced here: 101 us
  blocking collectives  72.3 us (71%)
  starting transfers between devices  9.81 us (10%)
  waiting for transfers between devices  7.96 us (8%)
  Pallas kernels  7.78 us (8%)
  local copies, waits for them, and re-layouts  1.75 us (2%)
  other arithmetic  1.6 us (2%)
    all_to_all x1, blocking collectives, on_device(): lax.all_to_all(jnp.broadcast_to(both, (nh * nz,) + both.shape), ('half',...  50.6 us
    all_to_all x1, blocking collectives, on_device(): parts = lax.all_to_all(parts, ('half', 'zh'), 0, 0, tiled=True)  21.7 us
    ppermute x3, starting transfers between devices, handed_on(): return lax.ppermute(block, ('section', 'half', 'odd'), route)  9.81 us
    ppermute x3, waiting for transfers between devices, handed_on(): return lax.ppermute(block, ('section', 'half', 'odd'), route)  7.96 us
    pallas_call x1, Pallas kernels, first(): pl.pallas_call(first_kernel, out_shape=[jax.ShapeDtypeStruct((tokens, wid...  4.48 us
    pallas_call x1, Pallas kernels, second(): pl.pallas_call(second_kernel, out_shape=jax.ShapeDtypeStruct((tokens, wid...  3.3 us
  transfers between devices with their start and end apart: 3, of which 2 were waited for; matrix products, arithmetic and copies ran while one was open for 0% of the time, Pallas kernels for 8%

profile of v4, /device:TPU:71, one launch (start us, length us, event | category | flops | bytes accessed | tf_op | source)
XLA Modules:
  0.0 101.3 jit_solution(14462612900248197490)
XLA Ops:
  0.0 0.8 pad_maximum_fusion
  0.8 50.6 %all_to_all.10.near_ref = bf16[16,8,2560]{2,1,0:T(8,128)(2,1)S(1)} all-to-all(bf16[16,8,2560]{2,1,0:T(8,128)(2,1)S(1)} %broadcast_in_dim.6), channel_id=1, replica_groups=mesh['section'=24,'half'=4,'odd'=2,'zh'=4] {'half','zh'}, dimensions={0} | all-to-all | bytes 1310720 | tf_op jit(solution)/shard_map/all_to_all | solution.py:131
  51.5 2.6 %collective-permute-start.1 = (bf16[16,8,2560]{2,1,0:T(8,128)(2,1)S(1)}, bf16[16,8,2560]{2,1,0:T(8,128)(2,1)S(1)}, u32[]{:S(2)}, u32[]{:S(2)}) collective-permute-start(bf16[16,8,2560]{2,1,0:T(8,128)(2,1)S(1)} %all_to_all.10.near_ref), channel_id=1, source_target_pairs={{0,4},{4,0},{8,12},{12,8},{16,20},{20,16},{24,28},{28,24},{32,60},... | collective-permute-start | bytes 1966088 | tf_op jit(solution)/shard_map/ppermute | solution.py:22
  54.1 0.0 copy-start
  54.1 1.6 %copy-done = bf16[2560,432]{0,1:T(8,128)(2,1)S(1)} copy-done((bf16[2560,432]{0,1:T(8,128)(2,1)S(1)}, bf16[2560,432]{0,1:T(8,128)(2,1)}, u32[]{:S(2)}) %copy-start) | copy-done | bytes 2211864
  55.7 0.0 copy-start.1
  55.7 4.5 %shard_map.55 = (bf16[64,2560]{1,0:T(8,128)(2,1)S(1)}, bf16[432,2560]{1,0:T(8,128)(2,1)S(1)}, bf16[432,2560]{1,0:T(8,128)(2,1)S(1)}) custom-call(bf16[16,8,2560]{2,1,0:T(8,128)(2,1)S(1)} %all_to_all.10.near_ref, bf16[432,2560]{1,0:T(8,128)(2,1)S(1)} %bitcast.5, bf16[432,2560]{1,0:T(8,128)(2,1)} %bitcast.7, bf16[432,2560]{1,0:T(8,128)(2,1)} %w_down_hbm.1), custom_call_target="tpu_custom_call" | custom-call | flops 707788800 | bytes 7290880 | tf_op jit(solution)/shard_map/pallas_call | solution.py:78
  60.2 3.6 %collective-permute-start = (bf16[64,2560]{1,0:T(8,128)(2,1)S(1)}, bf16[64,2560]{1,0:T(8,128)(2,1)S(1)}, u32[]{:S(2)}, u32[]{:S(2)}) collective-permute-start(bf16[64,2560]{1,0:T(8,128)(2,1)S(1)} %get-tuple-element.8.kept_ref), channel_id=1, source_target_pairs={{32,0},{36,4},{40,8},{44,12},{48,16},{52,20},{56,24},{60,28},{64,3... | collective-permute-start | bytes 983048 | tf_op jit(solution)/shard_map/ppermute | solution.py:22
  63.8 0.2 collective-permute-done.1.near_ref
  64.0 0.0 copy-done.1
  64.0 3.3 %shard_map.57 = bf16[64,2560]{1,0:T(8,128)(2,1)S(1)} custom-call(bf16[16,8,2560]{2,1,0:T(8,128)(2,1)S(1)} %collective-permute-done.1.near_ref, bf16[432,2560]{1,0:T(8,128)(2,1)S(1)} %bitcast.6, bf16[432,2560]{1,0:T(8,128)(2,1)S(1)} %get-tuple-element.9.w_up_ref, bf16[432,2560]{1,0:T(8,128)(2,1)S(1)} %get-tuple-element.10.w_down_ref, ...), custom_call_target="tpu_custom_call" | custom-call | flops 707788800 | bytes 7290880 | tf_op jit(solution)/shard_map/pallas_call | solution.py:102
  67.3 3.6 %collective-permute-start.2 = (bf16[64,2560]{1,0:T(8,128)(2,1)S(1)}, bf16[64,2560]{1,0:T(8,128)(2,1)S(1)}, u32[]{:S(2)}, u32[]{:S(2)}) collective-permute-start(bf16[64,2560]{1,0:T(8,128)(2,1)S(1)} %shard_map.57), channel_id=1, source_target_pairs={{32,28},{36,8},{40,4},{44,16},{48,12},{52,24},{56,20},{60,0},{64,3... | collective-permute-start | bytes 983048 | tf_op jit(solution)/shard_map/ppermute | solution.py:22
  70.9 0.0 collective-permute-done
  70.9 7.8 %collective-permute-done.2 = bf16[64,2560]{1,0:T(8,128)(2,1)S(1)} collective-permute-done((bf16[64,2560]{1,0:T(8,128)(2,1)S(1)}, bf16[64,2560]{1,0:T(8,128)(2,1)S(1)}, u32[]{:S(2)}, u32[]{:S(2)}) %collective-permute-start.2) | collective-permute-done | bytes 327712 | tf_op jit(solution)/shard_map/ppermute | solution.py:22
  78.7 0.1 add_convert_fusion
  78.8 0.1 reshape.3
  78.9 21.7 %all_to_all.11 = bf16[16,4,2560]{2,1,0:T(4,128)(2,1)S(1)} all-to-all(bf16[16,4,2560]{2,1,0:T(4,128)(2,1)S(1)} %reshape.3), channel_id=1, replica_groups=mesh['section'=24,'half'=4,'odd'=2,'zh'=4] {'half','zh'}, dimensions={0} | all-to-all | bytes 655360 | tf_op jit(solution)/shard_map/all_to_all | solution.py:142
  100.6 0.8 reduce_sum.12
  (2 shorter events, 0.0 us)
Async XLA Ops:
  51.5 12.5 %collective-permute-start.1 = (bf16[16,8,2560]{2,1,0:T(8,128)(2,1)S(1)}, bf16[16,8,2560]{2,1,0:T(8,128)(2,1)S(1)}, u32[]{:S(2)}, u32[]{:S(2)}) collective-permute-start(bf16[16,8,2560]{2,1,0:T(8,128)(2,1)S(1)} %all_to_all.10.near_ref), channel_id=1, source_target_pairs={{0,4},{4,0},{8,12},{12,8},{16,20},{20,16},{24,28},{28,24},{32,60},... | collective-permute-start | bytes 1966088 | tf_op jit(solution)/shard_map/ppermute | solution.py:22
  54.1 1.6 %copy-start = (bf16[2560,432]{0,1:T(8,128)(2,1)S(1)}, bf16[2560,432]{0,1:T(8,128)(2,1)}, u32[]{:S(2)}) copy-start(bf16[2560,432]{0,1:T(8,128)(2,1)} %param.7) | copy-start | bytes 6635524
  55.7 8.3 %copy-start.1 = (bf16[2560,432]{0,1:T(8,128)(2,1)S(1)}, bf16[2560,432]{0,1:T(8,128)(2,1)}, u32[]{:S(2)}) copy-start(bf16[2560,432]{0,1:T(8,128)(2,1)} %param.7) | copy-start | bytes 6635524
  60.2 10.7 %collective-permute-start = (bf16[64,2560]{1,0:T(8,128)(2,1)S(1)}, bf16[64,2560]{1,0:T(8,128)(2,1)S(1)}, u32[]{:S(2)}, u32[]{:S(2)}) collective-permute-start(bf16[64,2560]{1,0:T(8,128)(2,1)S(1)} %get-tuple-element.8.kept_ref), channel_id=1, source_target_pairs={{32,0},{36,4},{40,8},{44,12},{48,16},{52,20},{56,24},{60,28},{64,3... | collective-permute-start | bytes 983048 | tf_op jit(solution)/shard_map/ppermute | solution.py:22
  67.3 11.4 %collective-permute-start.2 = (bf16[64,2560]{1,0:T(8,128)(2,1)S(1)}, bf16[64,2560]{1,0:T(8,128)(2,1)S(1)}, u32[]{:S(2)}, u32[]{:S(2)}) collective-permute-start(bf16[64,2560]{1,0:T(8,128)(2,1)S(1)} %shard_map.57), channel_id=1, source_target_pairs={{32,28},{36,8},{40,4},{44,16},{48,12},{52,24},{56,20},{60,0},{64,3... | collective-permute-start | bytes 983048 | tf_op jit(solution)/shard_map/ppermute | solution.py:22

commit v5 on v4

--- a/solution.py
+++ b/solution.py
@@ -27,13 +27,9 @@
 
 
 def sorted_rows(near_ref):
-    n, eight, width = near_ref.shape
-    pairs = near_ref[...].astype(jnp.float32).reshape(n // 2, 2, eight, width)
-    even, odd = pairs[:, 0], pairs[:, 1]
-    upper = lax.broadcasted_iota(jnp.int32, even.shape, 1) < eight // 2
-    x = jnp.where(upper, even, pltpu.roll(odd, eight // 2, 1))
-    g = jnp.where(upper, pltpu.roll(even, eight // 2, 1), odd)
-    return [r.reshape(n * eight // 2, width).astype(near_ref.dtype) for r in (x, g)]
+    n, both, width = near_ref.shape
+    x, g = near_ref[:, : both // 2, :], near_ref[:, both // 2 :, :]
+    return [r.reshape(n * both // 2, width) for r in (x, g)]
 
 
 def gate_factors(gate, up):
@@ -128,15 +124,16 @@
     nh, nz = lax.axis_size("half"), lax.axis_size("zh")
     both = jnp.concatenate([inputs[0], out_grad[0]], axis=0)
     w_gate, w_up = w_gate.T, w_up.T
-    near = lax.all_to_all(
-        jnp.broadcast_to(both, (nh * nz,) + both.shape), ("half", "zh"), 0, 0, tiled=True
-    )
-    other = handed_on(near, 1, 0)
+    close = lax.all_to_all(jnp.broadcast_to(both, (nz,) + both.shape), "zh", 0, 0, tiled=True)
+    close = close.reshape(nz, 2, rows, width).transpose(1, 0, 2, 3)
+    close = close.reshape(2 * nz * rows, width)
+    near = lax.all_gather(close, "half", axis=0)
+    other = handed_on(near, 1, 1)
     kept, w_up, w_down = first(near, w_gate, w_up, w_down)
     sent = handed_on(kept, 0, 1)
     token = turn(kept)
     lent = second(other, w_gate, w_up, w_down, token)
-    lent = handed_on(lent, 1, 1)
+    lent = handed_on(lent, 1, 0)
     total = sent.astype(jnp.float32) + lent.astype(jnp.float32)
     parts = total.astype(jnp.bfloat16).reshape(nh * nz, rows, width)
     parts = lax.all_to_all(parts, ("half", "zh"), 0, 0, tiled=True)

time: 102 us -> 99.4 us (0.975)
  the two profiles are of different devices: /device:TPU:71 before, /device:TPU:6 now
where the time goes in v5:
time: 99.4 us; the launch traced here: 99.1 us
  blocking collectives  71.7 us (72%)
  starting transfers between devices  9.04 us (9%)
  waiting for transfers between devices  8.64 us (9%)
  Pallas kernels  7.61 us (8%)
  other arithmetic  1.75 us (2%)
    all_to_all x1, blocking collectives, on_device(): lax.all_to_all(jnp.broadcast_to(both, (nz,) + both.shape), 'zh', 0, 0, ti...  27.8 us
    all_to_all x1, blocking collectives, on_device(): parts = lax.all_to_all(parts, ('half', 'zh'), 0, 0, tiled=True)  25.4 us
    all_gather x1, blocking collectives, on_device(): near = lax.all_gather(close, 'half', axis=0)  18.5 us
    ppermute x3, starting transfers between devices, handed_on(): return lax.ppermute(block, ('section', 'half', 'odd'), route)  9.04 us
    ppermute x3, waiting for transfers between devices, handed_on(): return lax.ppermute(block, ('section', 'half', 'odd'), route)  8.64 us
    pallas_call x1, Pallas kernels, first(): pl.pallas_call(first_kernel, out_shape=[jax.ShapeDtypeStruct((tokens, wid...  4.33 us
    pallas_call x1, Pallas kernels, second(): pl.pallas_call(second_kernel, out_shape=jax.ShapeDtypeStruct((tokens, wid...  3.27 us
  transfers between devices with their start and end apart: 3, of which 2 were waited for; matrix products, arithmetic and copies ran while one was open for 0% of the time, Pallas kernels for 8%

profile of v5, /device:TPU:6, one launch (start us, length us, event | category | flops | bytes accessed | tf_op | source)
XLA Modules:
  0.0 99.1 jit_solution(6123997371542826456)
XLA Ops:
  0.0 0.0 copy-start
  0.0 0.9 pad_maximum_fusion
  0.9 27.8 %all_to_all.10 = bf16[4,8,2560]{2,1,0:T(8,128)(2,1)S(1)} all-to-all(bf16[4,8,2560]{2,1,0:T(8,128)(2,1)S(1)} %broadcast_in_dim.6), channel_id=1, replica_groups=mesh['section'=24,'half'=4,'odd'=2,'zh'=4] {'zh'}, dimensions={0} | all-to-all | bytes 327680 | tf_op jit(solution)/shard_map/all_to_all | solution.py:127
  28.8 0.1 copy.8
  28.9 0.1 copy.9
  29.0 18.5 %all_gather.3.near_ref = bf16[4,32,2560]{2,1,0:T(8,128)(2,1)S(1)} all-gather(bf16[1,32,2560]{2,1,0:T(8,128)(2,1)S(1)} %all_gather_reshape.3), channel_id=1, replica_groups=mesh['section'=24,'half'=4,'odd'=2,'zh'=4] {'half'}, dimensions={0}, use_global_device_ids=true | all-gather | bytes 819200 | tf_op jit(solution)/shard_map/all_gather | solution.py:130
  47.5 1.9 %collective-permute-start.1 = (bf16[4,32,2560]{2,1,0:T(8,128)(2,1)S(1)}, bf16[4,32,2560]{2,1,0:T(8,128)(2,1)S(1)}, u32[]{:S(2)}, u32[]{:S(2)}) collective-permute-start(bf16[4,32,2560]{2,1,0:T(8,128)(2,1)S(1)} %all_gather.3.near_ref), channel_id=1, source_target_pairs={{32,28},{36,8},{40,4},{44,16},{48,12},{52,24},{56,20},{60,0},{64,3... | collective-permute-start | bytes 1966088 | tf_op jit(solution)/shard_map/ppermute | solution.py:22
  49.4 0.0 copy-done
  49.4 4.3 %shard_map.55 = (bf16[64,2560]{1,0:T(8,128)(2,1)S(1)}, bf16[432,2560]{1,0:T(8,128)(2,1)S(1)}, bf16[432,2560]{1,0:T(8,128)(2,1)S(1)}) custom-call(bf16[4,32,2560]{2,1,0:T(8,128)(2,1)S(1)} %all_gather.3.near_ref, bf16[432,2560]{1,0:T(8,128)(2,1)S(1)} %bitcast.8, bf16[432,2560]{1,0:T(8,128)(2,1)} %bitcast.10, bf16[432,2560]{1,0:T(8,128)(2,1)} %w_down_hbm.1), custom_call_target="tpu_custom_call" | custom-call | flops 707788800 | bytes 7290880 | tf_op jit(solution)/shard_map/pallas_call | solution.py:74
  53.8 4.8 %collective-permute-start = (bf16[64,2560]{1,0:T(8,128)(2,1)S(1)}, bf16[64,2560]{1,0:T(8,128)(2,1)S(1)}, u32[]{:S(2)}, u32[]{:S(2)}) collective-permute-start(bf16[64,2560]{1,0:T(8,128)(2,1)S(1)} %get-tuple-element.8.kept_ref), channel_id=1, source_target_pairs={{32,0},{36,4},{40,8},{44,12},{48,16},{52,20},{56,24},{60,28},{64,3... | collective-permute-start | bytes 983048 | tf_op jit(solution)/shard_map/ppermute | solution.py:22
  58.5 2.0 %collective-permute-done.1.near_ref = bf16[4,32,2560]{2,1,0:T(8,128)(2,1)S(1)} collective-permute-done((bf16[4,32,2560]{2,1,0:T(8,128)(2,1)S(1)}, bf16[4,32,2560]{2,1,0:T(8,128)(2,1)S(1)}, u32[]{:S(2)}, u32[]{:S(2)}) %collective-permute-start.1) | collective-permute-done | bytes 655392 | tf_op jit(solution)/shard_map/ppermute | solution.py:22
  60.6 3.3 %shard_map.57 = bf16[64,2560]{1,0:T(8,128)(2,1)S(1)} custom-call(bf16[4,32,2560]{2,1,0:T(8,128)(2,1)S(1)} %collective-permute-done.1.near_ref, bf16[432,2560]{1,0:T(8,128)(2,1)S(1)} %bitcast.9, bf16[432,2560]{1,0:T(8,128)(2,1)S(1)} %get-tuple-element.9.w_up_ref, bf16[432,2560]{1,0:T(8,128)(2,1)S(1)} %get-tuple-element.10.w_down_ref, ...), custom_call_target="tpu_custom_call" | custom-call | flops 707788800 | bytes 7290880 | tf_op jit(solution)/shard_map/pallas_call | solution.py:98
  63.9 2.4 %collective-permute-start.2 = (bf16[64,2560]{1,0:T(8,128)(2,1)S(1)}, bf16[64,2560]{1,0:T(8,128)(2,1)S(1)}, u32[]{:S(2)}, u32[]{:S(2)}) collective-permute-start(bf16[64,2560]{1,0:T(8,128)(2,1)S(1)} %shard_map.57), channel_id=1, source_target_pairs={{0,4},{4,0},{8,12},{12,8},{16,20},{20,16},{24,28},{28,24},{32,60},... | collective-permute-start | bytes 983048 | tf_op jit(solution)/shard_map/ppermute | solution.py:22
  66.2 0.0 collective-permute-done
  66.2 6.6 %collective-permute-done.2 = bf16[64,2560]{1,0:T(8,128)(2,1)S(1)} collective-permute-done((bf16[64,2560]{1,0:T(8,128)(2,1)S(1)}, bf16[64,2560]{1,0:T(8,128)(2,1)S(1)}, u32[]{:S(2)}, u32[]{:S(2)}) %collective-permute-start.2) | collective-permute-done | bytes 327712 | tf_op jit(solution)/shard_map/ppermute | solution.py:22
  72.8 0.1 add_convert_fusion
  72.9 0.1 reshape.7
  73.0 25.4 %all_to_all.11 = bf16[16,4,2560]{2,1,0:T(4,128)(2,1)S(1)} all-to-all(bf16[16,4,2560]{2,1,0:T(4,128)(2,1)S(1)} %reshape.7), channel_id=1, replica_groups=mesh['section'=24,'half'=4,'odd'=2,'zh'=4] {'half','zh'}, dimensions={0} | all-to-all | bytes 655360 | tf_op jit(solution)/shard_map/all_to_all | solution.py:139
  98.4 0.8 reduce_sum.12
  (3 shorter events, 0.1 us)
Async XLA Ops:
  0.0 49.4 %copy-start = (bf16[2560,432]{0,1:T(8,128)(2,1)S(1)}, bf16[2560,432]{0,1:T(8,128)(2,1)}, u32[]{:S(2)}) copy-start(bf16[2560,432]{0,1:T(8,128)(2,1)} %param.7) | copy-start | bytes 6635524
  47.5 13.1 %collective-permute-start.1 = (bf16[4,32,2560]{2,1,0:T(8,128)(2,1)S(1)}, bf16[4,32,2560]{2,1,0:T(8,128)(2,1)S(1)}, u32[]{:S(2)}, u32[]{:S(2)}) collective-permute-start(bf16[4,32,2560]{2,1,0:T(8,128)(2,1)S(1)} %all_gather.3.near_ref), channel_id=1, source_target_pairs={{32,28},{36,8},{40,4},{44,16},{48,12},{52,24},{56,20},{60,0},{64,3... | collective-permute-start | bytes 1966088 | tf_op jit(solution)/shard_map/ppermute | solution.py:22
  53.8 12.5 %collective-permute-start = (bf16[64,2560]{1,0:T(8,128)(2,1)S(1)}, bf16[64,2560]{1,0:T(8,128)(2,1)S(1)}, u32[]{:S(2)}, u32[]{:S(2)}) collective-permute-start(bf16[64,2560]{1,0:T(8,128)(2,1)S(1)} %get-tuple-element.8.kept_ref), channel_id=1, source_target_pairs={{32,0},{36,4},{40,8},{44,12},{48,16},{52,20},{56,24},{60,28},{64,3... | collective-permute-start | bytes 983048 | tf_op jit(solution)/shard_map/ppermute | solution.py:22
  63.9 9.0 %collective-permute-start.2 = (bf16[64,2560]{1,0:T(8,128)(2,1)S(1)}, bf16[64,2560]{1,0:T(8,128)(2,1)S(1)}, u32[]{:S(2)}, u32[]{:S(2)}) collective-permute-start(bf16[64,2560]{1,0:T(8,128)(2,1)S(1)} %shard_map.57), channel_id=1, source_target_pairs={{0,4},{4,0},{8,12},{12,8},{16,20},{20,16},{24,28},{28,24},{32,60},... | collective-permute-start | bytes 983048 | tf_op jit(solution)/shard_map/ppermute | solution.py:22

commit v6 on v5

--- a/solution.py
+++ b/solution.py
@@ -105,6 +105,34 @@
     )(near, *operands)
 
 
+def spread_kernel(inputs_hbm, out_grad_hbm, out_ref, inputs_ref, out_grad_ref, here):
+    copies = [
+        pltpu.make_async_copy(inputs_hbm, inputs_ref, here.at[0]),
+        pltpu.make_async_copy(out_grad_hbm, out_grad_ref, here.at[1]),
+    ]
+    for c in copies:
+        c.start()
+    for c in copies:
+        c.wait()
+    parts = [r[0].astype(jnp.float32) for r in (inputs_ref, out_grad_ref)]
+    both = jnp.concatenate(parts, axis=0).astype(out_ref.dtype)
+    for i in range(out_ref.shape[0]):
+        out_ref[i] = both
+
+
+def spread(inputs, out_grad, copies):
+    rows, width = inputs.shape[1:]
+    return pl.pallas_call(
+        spread_kernel,
+        out_shape=jax.ShapeDtypeStruct((copies, 2 * rows, width), inputs.dtype),
+        in_specs=[pl.BlockSpec(memory_space=pltpu.HBM)] * 2,
+        out_specs=VMEM,
+        scratch_shapes=[pltpu.VMEM(inputs.shape, inputs.dtype)] * 2
+        + [pltpu.SemaphoreType.DMA((2,))],
+        compiler_params=PARAMS,
+    )(*(pltpu.with_memory_space_constraint(a, pltpu.HBM) for a in (inputs, out_grad)))
+
+
 def turn_kernel(kept_ref, token_ref):
     token_ref[...] = kept_ref[: token_ref.shape[0], : token_ref.shape[1]].astype(token_ref.dtype)
 
@@ -122,9 +150,8 @@
 def on_device(inputs, out_grad, w_gate, w_up, w_down):
     rows, width = inputs.shape[1:]
     nh, nz = lax.axis_size("half"), lax.axis_size("zh")
-    both = jnp.concatenate([inputs[0], out_grad[0]], axis=0)
     w_gate, w_up = w_gate.T, w_up.T
-    close = lax.all_to_all(jnp.broadcast_to(both, (nz,) + both.shape), "zh", 0, 0, tiled=True)
+    close = lax.all_to_all(spread(inputs, out_grad, nz), "zh", 0, 0, tiled=True)
     close = close.reshape(nz, 2, rows, width).transpose(1, 0, 2, 3)
     close = close.reshape(2 * nz * rows, width)
     near = lax.all_gather(close, "half", axis=0)

time: 99.4 us -> 99.3 us (level)
  no operation moved by 1% of the time
where the time goes in v6:
time: 99.3 us; the launch traced here: 99.1 us
  blocking collectives  71.7 us (72%)
  starting transfers between devices  9.07 us (9%)
  waiting for transfers between devices  8.61 us (9%)
  Pallas kernels  8.53 us (9%)
    all_to_all x1, blocking collectives, on_device(): close = lax.all_to_all(spread(inputs, out_grad, nz), 'zh', 0, 0, tiled=True)  27.8 us
    all_to_all x1, blocking collectives, on_device(): parts = lax.all_to_all(parts, ('half', 'zh'), 0, 0, tiled=True)  25.4 us
    all_gather x1, blocking collectives, on_device(): near = lax.all_gather(close, 'half', axis=0)  18.5 us
    ppermute x3, starting transfers between devices, handed_on(): return lax.ppermute(block, ('section', 'half', 'odd'), route)  9.07 us
    ppermute x3, waiting for transfers between devices, handed_on(): return lax.ppermute(block, ('section', 'half', 'odd'), route)  8.61 us
    pallas_call x1, Pallas kernels, first(): pl.pallas_call(first_kernel, out_shape=[jax.ShapeDtypeStruct((tokens, wid...  4.33 us
    pallas_call x1, Pallas kernels, second(): pl.pallas_call(second_kernel, out_shape=jax.ShapeDtypeStruct((tokens, wid...  3.27 us
  transfers between devices with their start and end apart: 3, of which 2 were waited for; matrix products, arithmetic and copies ran while one was open for 0% of the time, Pallas kernels for 8%

profile of v6, /device:TPU:6, one launch (start us, length us, event | category | flops | bytes accessed | tf_op | source)
XLA Modules:
  0.0 99.1 jit_solution(15120473938920416851)
XLA Ops:
  0.0 0.0 copy-start
  0.0 0.9 shard_map.55
  0.9 27.8 %all_to_all.10 = bf16[4,8,2560]{2,1,0:T(8,128)(2,1)S(1)} all-to-all(bf16[4,8,2560]{2,1,0:T(8,128)(2,1)S(1)} %shard_map.55), channel_id=1, replica_groups=mesh['section'=24,'half'=4,'odd'=2,'zh'=4] {'zh'}, dimensions={0} | all-to-all | bytes 327680 | tf_op jit(solution)/shard_map/all_to_all | solution.py:154
  28.8 0.1 copy.7
  28.9 18.5 %all_gather.3.near_ref = bf16[4,32,2560]{2,1,0:T(8,128)(2,1)S(1)} all-gather(bf16[1,32,2560]{2,1,0:T(8,128)(2,1)S(1)} %all_gather_reshape.3), channel_id=1, replica_groups=mesh['section'=24,'half'=4,'odd'=2,'zh'=4] {'half'}, dimensions={0}, use_global_device_ids=true | all-gather | bytes 819200 | tf_op jit(solution)/shard_map/all_gather | solution.py:157
  47.4 1.9 %collective-permute-start.1 = (bf16[4,32,2560]{2,1,0:T(8,128)(2,1)S(1)}, bf16[4,32,2560]{2,1,0:T(8,128)(2,1)S(1)}, u32[]{:S(2)}, u32[]{:S(2)}) collective-permute-start(bf16[4,32,2560]{2,1,0:T(8,128)(2,1)S(1)} %all_gather.3.near_ref), channel_id=1, source_target_pairs={{32,28},{36,8},{40,4},{44,16},{48,12},{52,24},{56,20},{60,0},{64,3... | collective-permute-start | bytes 1966088 | tf_op jit(solution)/shard_map/ppermute | solution.py:22
  49.3 0.0 copy-done
  49.4 4.3 %shard_map.56 = (bf16[64,2560]{1,0:T(8,128)(2,1)S(1)}, bf16[432,2560]{1,0:T(8,128)(2,1)S(1)}, bf16[432,2560]{1,0:T(8,128)(2,1)S(1)}) custom-call(bf16[4,32,2560]{2,1,0:T(8,128)(2,1)S(1)} %all_gather.3.near_ref, bf16[432,2560]{1,0:T(8,128)(2,1)S(1)} %bitcast.4, bf16[432,2560]{1,0:T(8,128)(2,1)} %bitcast.6, bf16[432,2560]{1,0:T(8,128)(2,1)} %w_down_hbm.1), custom_call_target="tpu_custom_call" | custom-call | flops 707788800 | bytes 7290880 | tf_op jit(solution)/shard_map/pallas_call | solution.py:74
  53.7 4.8 %collective-permute-start = (bf16[64,2560]{1,0:T(8,128)(2,1)S(1)}, bf16[64,2560]{1,0:T(8,128)(2,1)S(1)}, u32[]{:S(2)}, u32[]{:S(2)}) collective-permute-start(bf16[64,2560]{1,0:T(8,128)(2,1)S(1)} %get-tuple-element.8.kept_ref), channel_id=1, source_target_pairs={{32,0},{36,4},{40,8},{44,12},{48,16},{52,20},{56,24},{60,28},{64,3... | collective-permute-start | bytes 983048 | tf_op jit(solution)/shard_map/ppermute | solution.py:22
  58.5 2.0 %collective-permute-done.1.near_ref = bf16[4,32,2560]{2,1,0:T(8,128)(2,1)S(1)} collective-permute-done((bf16[4,32,2560]{2,1,0:T(8,128)(2,1)S(1)}, bf16[4,32,2560]{2,1,0:T(8,128)(2,1)S(1)}, u32[]{:S(2)}, u32[]{:S(2)}) %collective-permute-start.1) | collective-permute-done | bytes 655392 | tf_op jit(solution)/shard_map/ppermute | solution.py:22
  60.5 3.3 %shard_map.58 = bf16[64,2560]{1,0:T(8,128)(2,1)S(1)} custom-call(bf16[4,32,2560]{2,1,0:T(8,128)(2,1)S(1)} %collective-permute-done.1.near_ref, bf16[432,2560]{1,0:T(8,128)(2,1)S(1)} %bitcast.5, bf16[432,2560]{1,0:T(8,128)(2,1)S(1)} %get-tuple-element.9.w_up_ref, bf16[432,2560]{1,0:T(8,128)(2,1)S(1)} %get-tuple-element.10.w_down_ref, ...), custom_call_target="tpu_custom_call" | custom-call | flops 707788800 | bytes 7290880 | tf_op jit(solution)/shard_map/pallas_call | solution.py:98
  63.8 2.4 %collective-permute-start.2 = (bf16[64,2560]{1,0:T(8,128)(2,1)S(1)}, bf16[64,2560]{1,0:T(8,128)(2,1)S(1)}, u32[]{:S(2)}, u32[]{:S(2)}) collective-permute-start(bf16[64,2560]{1,0:T(8,128)(2,1)S(1)} %shard_map.58), channel_id=1, source_target_pairs={{0,4},{4,0},{8,12},{12,8},{16,20},{20,16},{24,28},{28,24},{32,60},... | collective-permute-start | bytes 983048 | tf_op jit(solution)/shard_map/ppermute | solution.py:22
  66.2 0.0 collective-permute-done
  66.2 6.6 %collective-permute-done.2 = bf16[64,2560]{1,0:T(8,128)(2,1)S(1)} collective-permute-done((bf16[64,2560]{1,0:T(8,128)(2,1)S(1)}, bf16[64,2560]{1,0:T(8,128)(2,1)S(1)}, u32[]{:S(2)}, u32[]{:S(2)}) %collective-permute-start.2) | collective-permute-done | bytes 327712 | tf_op jit(solution)/shard_map/ppermute | solution.py:22
  72.8 0.1 add_convert_fusion
  72.8 0.1 reshape.7
  72.9 25.4 %all_to_all.11 = bf16[16,4,2560]{2,1,0:T(4,128)(2,1)S(1)} all-to-all(bf16[16,4,2560]{2,1,0:T(4,128)(2,1)S(1)} %reshape.7), channel_id=1, replica_groups=mesh['section'=24,'half'=4,'odd'=2,'zh'=4] {'half','zh'}, dimensions={0} | all-to-all | bytes 655360 | tf_op jit(solution)/shard_map/all_to_all | solution.py:166
  98.3 0.8 reduce_sum.12
  (3 shorter events, 0.1 us)
Async XLA Ops:
  0.0 49.3 %copy-start = (bf16[2560,432]{0,1:T(8,128)(2,1)S(1)}, bf16[2560,432]{0,1:T(8,128)(2,1)}, u32[]{:S(2)}) copy-start(bf16[2560,432]{0,1:T(8,128)(2,1)} %param.7) | copy-start | bytes 6635524
  47.4 13.1 %collective-permute-start.1 = (bf16[4,32,2560]{2,1,0:T(8,128)(2,1)S(1)}, bf16[4,32,2560]{2,1,0:T(8,128)(2,1)S(1)}, u32[]{:S(2)}, u32[]{:S(2)}) collective-permute-start(bf16[4,32,2560]{2,1,0:T(8,128)(2,1)S(1)} %all_gather.3.near_ref), channel_id=1, source_target_pairs={{32,28},{36,8},{40,4},{44,16},{48,12},{52,24},{56,20},{60,0},{64,3... | collective-permute-start | bytes 1966088 | tf_op jit(solution)/shard_map/ppermute | solution.py:22
  53.7 12.5 %collective-permute-start = (bf16[64,2560]{1,0:T(8,128)(2,1)S(1)}, bf16[64,2560]{1,0:T(8,128)(2,1)S(1)}, u32[]{:S(2)}, u32[]{:S(2)}) collective-permute-start(bf16[64,2560]{1,0:T(8,128)(2,1)S(1)} %get-tuple-element.8.kept_ref), channel_id=1, source_target_pairs={{32,0},{36,4},{40,8},{44,12},{48,16},{52,20},{56,24},{60,28},{64,3... | collective-permute-start | bytes 983048 | tf_op jit(solution)/shard_map/ppermute | solution.py:22
  63.8 9.0 %collective-permute-start.2 = (bf16[64,2560]{1,0:T(8,128)(2,1)S(1)}, bf16[64,2560]{1,0:T(8,128)(2,1)S(1)}, u32[]{:S(2)}, u32[]{:S(2)}) collective-permute-start(bf16[64,2560]{1,0:T(8,128)(2,1)S(1)} %shard_map.58), channel_id=1, source_target_pairs={{0,4},{4,0},{8,12},{12,8},{16,20},{20,16},{24,28},{28,24},{32,60},... | collective-permute-start | bytes 983048 | tf_op jit(solution)/shard_map/ppermute | solution.py:22

commit v7 on v6

--- a/solution.py
+++ b/solution.py
@@ -133,6 +133,22 @@
     )(*(pltpu.with_memory_space_constraint(a, pltpu.HBM) for a in (inputs, out_grad)))
 
 
+def add_kernel(a_ref, b_ref, out_ref):
+    total = a_ref[...].astype(jnp.float32) + b_ref[...].astype(jnp.float32)
+    out_ref[...] = total.reshape(out_ref.shape).astype(out_ref.dtype)
+
+
+def added(a, b, rows):
+    tokens, width = a.shape
+    return pl.pallas_call(
+        add_kernel,
+        out_shape=jax.ShapeDtypeStruct((tokens // rows, rows, width), a.dtype),
+        in_specs=[VMEM] * 2,
+        out_specs=VMEM,
+        compiler_params=PARAMS,
+    )(a, b)
+
+
 def turn_kernel(kept_ref, token_ref):
     token_ref[...] = kept_ref[: token_ref.shape[0], : token_ref.shape[1]].astype(token_ref.dtype)
 
@@ -149,7 +165,7 @@
 
 def on_device(inputs, out_grad, w_gate, w_up, w_down):
     rows, width = inputs.shape[1:]
-    nh, nz = lax.axis_size("half"), lax.axis_size("zh")
+    nz = lax.axis_size("zh")
     w_gate, w_up = w_gate.T, w_up.T
     close = lax.all_to_all(spread(inputs, out_grad, nz), "zh", 0, 0, tiled=True)
     close = close.reshape(nz, 2, rows, width).transpose(1, 0, 2, 3)
@@ -161,8 +177,7 @@
     token = turn(kept)
     lent = second(other, w_gate, w_up, w_down, token)
     lent = handed_on(lent, 1, 0)
-    total = sent.astype(jnp.float32) + lent.astype(jnp.float32)
-    parts = total.astype(jnp.bfloat16).reshape(nh * nz, rows, width)
+    parts = added(sent, lent, rows)
     parts = lax.all_to_all(parts, ("half", "zh"), 0, 0, tiled=True)
     in_grad = jnp.sum(parts.astype(jnp.float32), axis=0).astype(jnp.bfloat16)
     return in_grad[None]

time: 99.3 us -> 99.3 us (level)
  no operation moved by 1% of the time
where the time goes in v7:
time: 99.3 us; the launch traced here: 99.1 us
  blocking collectives  71.7 us (72%)
  starting transfers between devices  9.07 us (9%)
  Pallas kernels  8.69 us (9%)
  waiting for transfers between devices  8.61 us (9%)
    all_to_all x1, blocking collectives, on_device(): close = lax.all_to_all(spread(inputs, out_grad, nz), 'zh', 0, 0, tiled=True)  27.8 us
    all_to_all x1, blocking collectives, on_device(): parts = lax.all_to_all(parts, ('half', 'zh'), 0, 0, tiled=True)  25.4 us
    all_gather x1, blocking collectives, on_device(): near = lax.all_gather(close, 'half', axis=0)  18.5 us
    ppermute x3, starting transfers between devices, handed_on(): return lax.ppermute(block, ('section', 'half', 'odd'), route)  9.07 us
    ppermute x3, waiting for transfers between devices, handed_on(): return lax.ppermute(block, ('section', 'half', 'odd'), route)  8.61 us
    pallas_call x1, Pallas kernels, first(): pl.pallas_call(first_kernel, out_shape=[jax.ShapeDtypeStruct((tokens, wid...  4.33 us
    pallas_call x1, Pallas kernels, second(): pl.pallas_call(second_kernel, out_shape=jax.ShapeDtypeStruct((tokens, wid...  3.27 us
  transfers between devices with their start and end apart: 3, of which 2 were waited for; matrix products, arithmetic and copies ran while one was open for 0% of the time, Pallas kernels for 8%

profile of v7, /device:TPU:6, one launch (start us, length us, event | category | flops | bytes accessed | tf_op | source)
XLA Modules:
  0.0 99.1 jit_solution(12183850677996026677)
XLA Ops:
  0.0 0.0 copy-start
  0.0 0.9 shard_map.55
  0.9 27.8 %all_to_all.10 = bf16[4,8,2560]{2,1,0:T(8,128)(2,1)S(1)} all-to-all(bf16[4,8,2560]{2,1,0:T(8,128)(2,1)S(1)} %shard_map.55), channel_id=1, replica_groups=mesh['section'=24,'half'=4,'odd'=2,'zh'=4] {'zh'}, dimensions={0} | all-to-all | bytes 327680 | tf_op jit(solution)/shard_map/all_to_all | solution.py:170
  28.8 0.1 copy.7
  28.9 18.5 %all_gather.3.near_ref = bf16[4,32,2560]{2,1,0:T(8,128)(2,1)S(1)} all-gather(bf16[1,32,2560]{2,1,0:T(8,128)(2,1)S(1)} %all_gather_reshape.3), channel_id=1, replica_groups=mesh['section'=24,'half'=4,'odd'=2,'zh'=4] {'half'}, dimensions={0}, use_global_device_ids=true | all-gather | bytes 819200 | tf_op jit(solution)/shard_map/all_gather | solution.py:173
  47.4 1.9 %collective-permute-start.1 = (bf16[4,32,2560]{2,1,0:T(8,128)(2,1)S(1)}, bf16[4,32,2560]{2,1,0:T(8,128)(2,1)S(1)}, u32[]{:S(2)}, u32[]{:S(2)}) collective-permute-start(bf16[4,32,2560]{2,1,0:T(8,128)(2,1)S(1)} %all_gather.3.near_ref), channel_id=1, source_target_pairs={{32,28},{36,8},{40,4},{44,16},{48,12},{52,24},{56,20},{60,0},{64,3... | collective-permute-start | bytes 1966088 | tf_op jit(solution)/shard_map/ppermute | solution.py:22
  49.3 0.0 copy-done
  49.4 4.3 %shard_map.56 = (bf16[64,2560]{1,0:T(8,128)(2,1)S(1)}, bf16[432,2560]{1,0:T(8,128)(2,1)S(1)}, bf16[432,2560]{1,0:T(8,128)(2,1)S(1)}) custom-call(bf16[4,32,2560]{2,1,0:T(8,128)(2,1)S(1)} %all_gather.3.near_ref, bf16[432,2560]{1,0:T(8,128)(2,1)S(1)} %bitcast.4, bf16[432,2560]{1,0:T(8,128)(2,1)} %bitcast.6, bf16[432,2560]{1,0:T(8,128)(2,1)} %w_down_hbm.1), custom_call_target="tpu_custom_call" | custom-call | flops 707788800 | bytes 7290880 | tf_op jit(solution)/shard_map/pallas_call | solution.py:74
  53.7 4.8 %collective-permute-start = (bf16[64,2560]{1,0:T(8,128)(2,1)S(1)}, bf16[64,2560]{1,0:T(8,128)(2,1)S(1)}, u32[]{:S(2)}, u32[]{:S(2)}) collective-permute-start(bf16[64,2560]{1,0:T(8,128)(2,1)S(1)} %get-tuple-element.8.kept_ref), channel_id=1, source_target_pairs={{32,0},{36,4},{40,8},{44,12},{48,16},{52,20},{56,24},{60,28},{64,3... | collective-permute-start | bytes 983048 | tf_op jit(solution)/shard_map/ppermute | solution.py:22
  58.5 2.0 %collective-permute-done.1.near_ref = bf16[4,32,2560]{2,1,0:T(8,128)(2,1)S(1)} collective-permute-done((bf16[4,32,2560]{2,1,0:T(8,128)(2,1)S(1)}, bf16[4,32,2560]{2,1,0:T(8,128)(2,1)S(1)}, u32[]{:S(2)}, u32[]{:S(2)}) %collective-permute-start.1) | collective-permute-done | bytes 655392 | tf_op jit(solution)/shard_map/ppermute | solution.py:22
  60.5 3.3 %shard_map.58 = bf16[64,2560]{1,0:T(8,128)(2,1)S(1)} custom-call(bf16[4,32,2560]{2,1,0:T(8,128)(2,1)S(1)} %collective-permute-done.1.near_ref, bf16[432,2560]{1,0:T(8,128)(2,1)S(1)} %bitcast.5, bf16[432,2560]{1,0:T(8,128)(2,1)S(1)} %get-tuple-element.9.w_up_ref, bf16[432,2560]{1,0:T(8,128)(2,1)S(1)} %get-tuple-element.10.w_down_ref, ...), custom_call_target="tpu_custom_call" | custom-call | flops 707788800 | bytes 7290880 | tf_op jit(solution)/shard_map/pallas_call | solution.py:98
  63.8 2.4 %collective-permute-start.2 = (bf16[64,2560]{1,0:T(8,128)(2,1)S(1)}, bf16[64,2560]{1,0:T(8,128)(2,1)S(1)}, u32[]{:S(2)}, u32[]{:S(2)}) collective-permute-start(bf16[64,2560]{1,0:T(8,128)(2,1)S(1)} %shard_map.58), channel_id=1, source_target_pairs={{0,4},{4,0},{8,12},{12,8},{16,20},{20,16},{24,28},{28,24},{32,60},... | collective-permute-start | bytes 983048 | tf_op jit(solution)/shard_map/ppermute | solution.py:22
  66.2 0.0 collective-permute-done.a_ref
  66.2 6.6 %collective-permute-done.2.b_ref = bf16[64,2560]{1,0:T(8,128)(2,1)S(1)} collective-permute-done((bf16[64,2560]{1,0:T(8,128)(2,1)S(1)}, bf16[64,2560]{1,0:T(8,128)(2,1)S(1)}, u32[]{:S(2)}, u32[]{:S(2)}) %collective-permute-start.2) | collective-permute-done | bytes 327712 | tf_op jit(solution)/shard_map/ppermute | solution.py:22
  72.8 0.2 shard_map.59
  72.9 25.4 %all_to_all.11 = bf16[16,4,2560]{2,1,0:T(4,128)(2,1)S(1)} all-to-all(bf16[16,4,2560]{2,1,0:T(4,128)(2,1)S(1)} %shard_map.59), channel_id=1, replica_groups=mesh['section'=24,'half'=4,'odd'=2,'zh'=4] {'half','zh'}, dimensions={0} | all-to-all | bytes 655360 | tf_op jit(solution)/shard_map/all_to_all | solution.py:181
  98.3 0.8 reduce_sum.12
  (3 shorter events, 0.1 us)
Async XLA Ops:
  0.0 49.3 %copy-start = (bf16[2560,432]{0,1:T(8,128)(2,1)S(1)}, bf16[2560,432]{0,1:T(8,128)(2,1)}, u32[]{:S(2)}) copy-start(bf16[2560,432]{0,1:T(8,128)(2,1)} %param.7) | copy-start | bytes 6635524
  47.4 13.1 %collective-permute-start.1 = (bf16[4,32,2560]{2,1,0:T(8,128)(2,1)S(1)}, bf16[4,32,2560]{2,1,0:T(8,128)(2,1)S(1)}, u32[]{:S(2)}, u32[]{:S(2)}) collective-permute-start(bf16[4,32,2560]{2,1,0:T(8,128)(2,1)S(1)} %all_gather.3.near_ref), channel_id=1, source_target_pairs={{32,28},{36,8},{40,4},{44,16},{48,12},{52,24},{56,20},{60,0},{64,3... | collective-permute-start | bytes 1966088 | tf_op jit(solution)/shard_map/ppermute | solution.py:22
  53.7 12.5 %collective-permute-start = (bf16[64,2560]{1,0:T(8,128)(2,1)S(1)}, bf16[64,2560]{1,0:T(8,128)(2,1)S(1)}, u32[]{:S(2)}, u32[]{:S(2)}) collective-permute-start(bf16[64,2560]{1,0:T(8,128)(2,1)S(1)} %get-tuple-element.8.kept_ref), channel_id=1, source_target_pairs={{32,0},{36,4},{40,8},{44,12},{48,16},{52,20},{56,24},{60,28},{64,3... | collective-permute-start | bytes 983048 | tf_op jit(solution)/shard_map/ppermute | solution.py:22
  63.8 9.0 %collective-permute-start.2 = (bf16[64,2560]{1,0:T(8,128)(2,1)S(1)}, bf16[64,2560]{1,0:T(8,128)(2,1)S(1)}, u32[]{:S(2)}, u32[]{:S(2)}) collective-permute-start(bf16[64,2560]{1,0:T(8,128)(2,1)S(1)} %shard_map.58), channel_id=1, source_target_pairs={{0,4},{4,0},{8,12},{12,8},{16,20},{20,16},{24,28},{28,24},{32,60},... | collective-permute-start | bytes 983048 | tf_op jit(solution)/shard_map/ppermute | solution.py:22
